TPU v7x, 32 devices: a whole 2x2x4 slice. The times are simulated.
32 devices in a mesh: batch: 4 (over y, core), expert: 8 (over z, x).
Axes of the slice: x: 2, y: 2, z: 4, core: 2. Of those that a mesh axis runs over, the one named last changes fastest.
Arguments:
- tokens: bfloat16 [32768, 768], P(('batch', 'expert')), may hold values from -10 to 10
- cotangent: bfloat16 [32768, 768], P(('batch', 'expert')), may hold values from -6 to 6
- lengths: int32 [32, 6], P(('batch', 'expert')), may hold values from 1 to 512, 1024 in all within a row
- routes: int32 [32768, 1], P(('batch', 'expert')), may hold values from 0 to 7; in each aligned block of 1024 rows (0 to 1023, 1024 to 2047, ...) at most 192 rows name the same one
- mixer_weight: bfloat16 [768, 2304], P(('batch', 'expert')), may hold values from -0.21875 to 0.21875
- output_weight: bfloat16 [768, 768], P(('batch', 'expert')), may hold values from -1.75 to 1.75
- first_gain: bfloat16 [768], P(('batch', 'expert')), may hold values from 0.5 to 1.5
- first_shift: bfloat16 [768], P(('batch', 'expert')), may hold values from -1.25 to 1.25
- second_gain: bfloat16 [768], P(('batch', 'expert')), may hold values from 0.5 to 1.5
- second_shift: bfloat16 [768], P(('batch', 'expert')), may hold values from -1.25 to 1.25
- router_weight: bfloat16 [768, 8], P(('batch', 'expert')), may hold values from -0.15625 to 0.15625
- inner_weight: bfloat16 [8, 768, 3072], P('expert'), may hold values from -0.21875 to 0.21875
- inner_bias: bfloat16 [8, 3072], P('expert'), may hold values from -1.75 to 1.75
- outer_weight: bfloat16 [8, 3072, 768], P('expert'), may hold values from -0.3125 to 0.3125
- outer_bias: bfloat16 [8, 768], P('expert'), may hold values from -1.75 to 1.75
Outputs:
- block_output: bfloat16 [32768, 768], P(('batch', 'expert'))
- input_grad: float32 [32768, 768], P(('batch', 'expert'))
- mixer_grad: float32 [768, 2304], P(('batch', 'expert'))
- output_grad: float32 [768, 768], P(('batch', 'expert'))
- first_gain_grad: float32 [768], P(('batch', 'expert'))
- first_shift_grad: float32 [768], P(('batch', 'expert'))
- second_gain_grad: float32 [768], P(('batch', 'expert'))
- second_shift_grad: float32 [768], P(('batch', 'expert'))
- router_grad: float32 [768, 8], P(('batch', 'expert'))
- inner_weight_grad: float32 [8, 768, 3072], P('expert')
- inner_bias_grad: float32 [8, 3072], P('expert')
- outer_weight_grad: float32 [8, 3072, 768], P('expert')
- outer_bias_grad: float32 [8, 768], P('expert')
- balance_loss: float32 [], replicated
- stream_rms: float32 [3], replicated
Inputs may be any that keep to these rules, and one draw needn't show every extreme that they name: Each row lists the lengths of the 6 sequences of one device's 1024 tokens, in order; they sum to 1024 and the largest is half of 1024. `routes`: among the 1024 rows of one device no expert is named more than 192 times, a bound that some block reaches.
All inputs are finite; a program needn't handle non-finite values.
Results may differ from a plain program's by a relative error of at most 0.013.
Values may be sent and summed in bfloat16 or wider, within the bound.
No kernel may reach another device: no remote copies, remote signals or barrier semaphores. Data moves between devices by JAX's collectives and lax.ppermute only.
A program may use at most 256 MiB of HBM per device.

v0:
```python
import jax
import jax.numpy as jnp
from jax import lax
from jax.sharding import PartitionSpec as P

HEADS = 12
HEAD_DIM = 64


EPSILON = 1e-05


def layer_norm(values, gain, shift):
    centre = values - jnp.mean(values, axis=-1, keepdims=True)
    spread = jnp.mean(centre * centre, axis=-1, keepdims=True)
    return centre * lax.rsqrt(spread + EPSILON) * gain + shift


def gelu_exact(values):
    return jax.nn.gelu(values, approximate=False)


def segment_of(lengths, rows_here):
    ends = jnp.cumsum(lengths[0])
    places = jnp.arange(rows_here, dtype=jnp.int32)
    return jnp.sum((places[:, None] >= ends[None, :]).astype(jnp.int32), axis=1)


def shards(
    tokens,
    cotangent,
    lengths,
    routes,
    mixer_weight,
    output_weight,
    first_gain,
    first_shift,
    second_gain,
    second_shift,
    router_weight,
    inner_weight,
    inner_bias,
    outer_weight,
    outer_bias,
):
    rows_here, model_width = tokens.shape
    gathered = (
        lax.all_gather(mixer_weight, ("batch", "expert"), axis=0, tiled=True),
        lax.all_gather(output_weight, ("batch", "expert"), axis=0, tiled=True),
        lax.all_gather(first_gain, ("batch", "expert"), axis=0, tiled=True),
        lax.all_gather(first_shift, ("batch", "expert"), axis=0, tiled=True),
        lax.all_gather(second_gain, ("batch", "expert"), axis=0, tiled=True),
        lax.all_gather(second_shift, ("batch", "expert"), axis=0, tiled=True),
        lax.all_gather(router_weight, ("batch", "expert"), axis=0, tiled=True),
    )
    (
        mixer_full,
        output_full,
        gain_low_one,
        shift_low_one,
        gain_low_two,
        shift_low_two,
        router_full,
    ) = gathered
    gain_one = gain_low_one.astype(jnp.float32)
    shift_one = shift_low_one.astype(jnp.float32)
    gain_two = gain_low_two.astype(jnp.float32)
    shift_two = shift_low_two.astype(jnp.float32)
    router_float = router_full.astype(jnp.float32)
    expert_count = router_full.shape[1]
    capacity = 3 * rows_here // (2 * expert_count)
    score_scale = HEAD_DIM ** (-0.5)
    block_rows = min(512, rows_here)
    block_count = rows_here // block_rows
    tokens_f = tokens.astype(jnp.float32)
    normed_one = layer_norm(tokens_f, gain_one, shift_one)
    normed_low = normed_one.astype(jnp.bfloat16)
    mixed = jnp.dot(normed_low, mixer_full, preferred_element_type=jnp.float32).astype(jnp.bfloat16)
    queries = mixed[:, :model_width].reshape(rows_here, HEADS, HEAD_DIM)
    keys_all = mixed[:, model_width : 2 * model_width].reshape(rows_here, HEADS, HEAD_DIM)
    values_all = mixed[:, 2 * model_width :].reshape(rows_here, HEADS, HEAD_DIM)
    segment = segment_of(lengths, rows_here)
    places = jnp.arange(rows_here, dtype=jnp.int32)

    def block_scores(offset):
        query_block = lax.dynamic_slice_in_dim(queries, offset, block_rows, 0)
        scores = (
            jnp.einsum("qhd,khd->hqk", query_block, keys_all, preferred_element_type=jnp.float32)
            * score_scale
        )
        rows_at = offset + jnp.arange(block_rows, dtype=jnp.int32)
        seg_rows = lax.dynamic_slice_in_dim(segment, offset, block_rows, 0)
        visible = (seg_rows[:, None] == segment[None, :]) & (places[None, :] <= rows_at[:, None])
        return (jnp.where(visible[None], scores, -1e30), query_block)

    def forward_block(number):
        scores, query_block = block_scores(number * block_rows)
        highest = jnp.max(scores, axis=-1, keepdims=True)
        exponent = jnp.exp(scores - highest)
        totals = jnp.sum(exponent, axis=-1, keepdims=True)
        attn_probs = exponent / totals
        log_total = highest + jnp.log(totals)
        attended = jnp.einsum(
            "hqk,khd->qhd",
            attn_probs.astype(jnp.bfloat16),
            values_all,
            preferred_element_type=jnp.float32,
        )
        return (attended, log_total, attn_probs)

    def forward_light(number):
        outputs = forward_block(number)
        return (outputs[0], outputs[1])

    numbers = jnp.arange(block_count, dtype=jnp.int32)
    attended, log_totals = lax.map(forward_light, numbers)
    attended_low = attended.reshape(rows_here, model_width).astype(jnp.bfloat16)
    attn_out = jnp.dot(attended_low, output_full, preferred_element_type=jnp.float32)
    stream = tokens_f + attn_out
    normed_two = layer_norm(stream, gain_two, shift_two)
    second_low = normed_two.astype(jnp.bfloat16)
    router_logits = jnp.dot(second_low, router_full, preferred_element_type=jnp.float32)
    chosen = routes[:, 0]
    hits = chosen[:, None] == jnp.arange(expert_count, dtype=jnp.int32)[None, :]
    onehot = hits.astype(jnp.float32)
    onehot_int = hits.astype(jnp.int32)
    gates = jax.nn.sigmoid(jnp.sum(router_logits * onehot, axis=1))
    ranks = jnp.sum((jnp.cumsum(onehot_int, axis=0) - onehot_int) * onehot_int, axis=1)
    targets = chosen * capacity + ranks

    def to_experts(rows_in):
        placed = (
            jnp.zeros((expert_count * capacity, model_width), jnp.bfloat16).at[targets].set(rows_in)
        )
        return placed.reshape(expert_count, capacity, model_width)

    received = lax.all_to_all(
        to_experts(second_low), "expert", split_axis=0, concat_axis=0, tiled=True
    ).reshape(expert_count * capacity, model_width)
    hidden_pre = jnp.dot(
        received, inner_weight[0], preferred_element_type=jnp.float32
    ) + inner_bias[0].astype(jnp.float32)
    hidden_act = gelu_exact(hidden_pre).astype(jnp.bfloat16)
    expert_out = (
        jnp.dot(hidden_act, outer_weight[0], preferred_element_type=jnp.float32)
        + outer_bias[0].astype(jnp.float32)
    ).astype(jnp.bfloat16)
    came_back = lax.all_to_all(
        expert_out.reshape(expert_count, capacity, model_width),
        "expert",
        split_axis=0,
        concat_axis=0,
        tiled=True,
    ).reshape(expert_count * capacity, model_width)
    picked = came_back[targets].astype(jnp.float32)
    moe_out = gates[:, None] * picked
    result = stream + moe_out
    local_counts = jnp.sum(onehot, axis=0)
    local_gates = jnp.sum(onehot * gates[:, None], axis=0)
    local_squares = jnp.stack(
        [jnp.sum(result * result), jnp.sum(attn_out * attn_out), jnp.sum(moe_out * moe_out)]
    )
    counts, gate_sums, squares = lax.psum(
        (local_counts, local_gates, local_squares), ("batch", "expert")
    )
    total_tokens = rows_here * lax.axis_size(("batch", "expert"))
    average = total_tokens / expert_count
    balance = jnp.sum((counts - average) / average * gate_sums) / total_tokens
    root_means = jnp.sqrt(squares / (total_tokens * model_width) + 1e-06)
    top_grad = cotangent.astype(jnp.float32)
    balance_terms = (counts - average) / (average * total_tokens)
    gate_grad = jnp.sum(top_grad * picked, axis=1) + jnp.sum(
        onehot * balance_terms[None, :], axis=1
    )
    out_row_grad = (gates[:, None] * top_grad).astype(jnp.bfloat16)
    out_grads = lax.all_to_all(
        to_experts(out_row_grad), "expert", split_axis=0, concat_axis=0, tiled=True
    ).reshape(expert_count * capacity, model_width)
    outer_b_grad = jnp.sum(out_grads.astype(jnp.float32), axis=0)
    outer_w_grad = jnp.einsum(
        "rf,rd->fd", hidden_act, out_grads, preferred_element_type=jnp.float32
    )
    act_grad = jnp.einsum(
        "rd,fd->rf", out_grads, outer_weight[0], preferred_element_type=jnp.float32
    )
    unused_value, gelu_back = jax.vjp(gelu_exact, hidden_pre)
    pre_grad = gelu_back(act_grad)[0].astype(jnp.bfloat16)
    inner_b_grad = jnp.sum(pre_grad.astype(jnp.float32), axis=0)
    inner_w_grad = jnp.einsum("rd,rf->df", received, pre_grad, preferred_element_type=jnp.float32)
    inner_w_sum, inner_b_sum, outer_w_sum, outer_b_sum = (
        lax.psum(inner_w_grad[None].astype(jnp.bfloat16), "batch").astype(jnp.float32),
        lax.psum(inner_b_grad[None].astype(jnp.bfloat16), "batch").astype(jnp.float32),
        lax.psum(outer_w_grad[None].astype(jnp.bfloat16), "batch").astype(jnp.float32),
        lax.psum(outer_b_grad[None].astype(jnp.bfloat16), "batch").astype(jnp.float32),
    )
    expert_in_grad = jnp.einsum(
        "rf,df->rd", pre_grad, inner_weight[0], preferred_element_type=jnp.float32
    ).astype(jnp.bfloat16)
    returned = lax.all_to_all(
        expert_in_grad.reshape(expert_count, capacity, model_width),
        "expert",
        split_axis=0,
        concat_axis=0,
        tiled=True,
    ).reshape(expert_count * capacity, model_width)
    returned_rows = returned[targets].astype(jnp.float32)
    logit_grad = gate_grad * gates * (1.0 - gates)
    route_grad = onehot * logit_grad[:, None]
    router_grad_w = jnp.einsum(
        "nd,ne->de", second_low.astype(jnp.float32), route_grad, precision=lax.Precision.HIGHEST
    )
    second_in_grad = returned_rows + jnp.dot(
        route_grad, router_float.T, precision=lax.Precision.HIGHEST
    )
    unused_two, second_back = jax.vjp(layer_norm, stream, gain_two, shift_two)
    stream_part, gain_two_grad, shift_two_grad = second_back(second_in_grad)
    stream_grad = top_grad + stream_part
    attn_grad = stream_grad.astype(jnp.bfloat16)
    output_grad_w = jnp.einsum(
        "nk,nd->kd", attended_low, attn_grad, preferred_element_type=jnp.float32
    )
    attended_grad = (
        jnp.einsum("nd,kd->nk", attn_grad, output_full, preferred_element_type=jnp.float32)
        .astype(jnp.bfloat16)
        .reshape(rows_here, HEADS, HEAD_DIM)
    )

    def backward_block(carry, number):
        key_acc, value_acc = carry
        offset = number * block_rows
        scores, query_block = block_scores(offset)
        attn_probs = jnp.exp(scores - log_totals[number])
        grad_block = lax.dynamic_slice_in_dim(attended_grad, offset, block_rows, 0)
        prob_grad = jnp.einsum(
            "qhd,khd->hqk", grad_block, values_all, preferred_element_type=jnp.float32
        )
        row_inner = jnp.sum(attn_probs * prob_grad, axis=-1, keepdims=True)
        score_grad = (attn_probs * (prob_grad - row_inner)).astype(jnp.bfloat16)
        query_grad = (
            jnp.einsum("hqk,khd->qhd", score_grad, keys_all, preferred_element_type=jnp.float32)
            * score_scale
        )
        key_acc = (
            key_acc
            + jnp.einsum(
                "hqk,qhd->khd", score_grad, query_block, preferred_element_type=jnp.float32
            )
            * score_scale
        )
        value_acc = value_acc + jnp.einsum(
            "hqk,qhd->khd",
            attn_probs.astype(jnp.bfloat16),
            grad_block,
            preferred_element_type=jnp.float32,
        )
        return ((key_acc, value_acc), query_grad)

    empty = jnp.zeros((rows_here, HEADS, HEAD_DIM), jnp.float32)
    (key_grads, value_grads), query_grads = lax.scan(backward_block, (empty, empty), numbers)
    mixed_grad = jnp.concatenate(
        [
            query_grads.reshape(rows_here, model_width),
            key_grads.reshape(rows_here, model_width),
            value_grads.reshape(rows_here, model_width),
        ],
        axis=1,
    ).astype(jnp.bfloat16)
    mixer_grad_w = jnp.einsum(
        "nd,ne->de", normed_low, mixed_grad, preferred_element_type=jnp.float32
    )
    normed_grad = jnp.einsum(
        "ne,de->nd", mixed_grad, mixer_full, preferred_element_type=jnp.float32
    )
    unused_one, first_back = jax.vjp(layer_norm, tokens_f, gain_one, shift_one)
    input_part, gain_one_grad, shift_one_grad = first_back(normed_grad)
    input_grad = stream_grad + input_part
    layer_sums = (
        lax.psum_scatter(mixer_grad_w, ("batch", "expert"), scatter_dimension=0, tiled=True),
        lax.psum_scatter(output_grad_w, ("batch", "expert"), scatter_dimension=0, tiled=True),
        lax.psum_scatter(gain_one_grad, ("batch", "expert"), scatter_dimension=0, tiled=True),
        lax.psum_scatter(shift_one_grad, ("batch", "expert"), scatter_dimension=0, tiled=True),
        lax.psum_scatter(gain_two_grad, ("batch", "expert"), scatter_dimension=0, tiled=True),
        lax.psum_scatter(shift_two_grad, ("batch", "expert"), scatter_dimension=0, tiled=True),
        lax.psum_scatter(router_grad_w, ("batch", "expert"), scatter_dimension=0, tiled=True),
    )
    return (
        result.astype(jnp.bfloat16),
        input_grad,
        layer_sums[0],
        layer_sums[1],
        layer_sums[2],
        layer_sums[3],
        layer_sums[4],
        layer_sums[5],
        layer_sums[6],
        inner_w_sum,
        inner_b_sum,
        outer_w_sum,
        outer_b_sum,
        balance,
        root_means,
    )


def solution(mesh):
    in_specs = (
        P(("batch", "expert"), None),
        P(("batch", "expert"), None),
        P(("batch", "expert"), None),
        P(("batch", "expert"), None),
        P(("batch", "expert"), None),
        P(("batch", "expert"), None),
        P(("batch", "expert")),
        P(("batch", "expert")),
        P(("batch", "expert")),
        P(("batch", "expert")),
        P(("batch", "expert"), None),
        P("expert", None, None),
        P("expert", None),
        P("expert", None, None),
        P("expert", None),
    )
    out_specs = (
        P(("batch", "expert"), None),
        P(("batch", "expert"), None),
        P(("batch", "expert"), None),
        P(("batch", "expert"), None),
        P(("batch", "expert")),
        P(("batch", "expert")),
        P(("batch", "expert")),
        P(("batch", "expert")),
        P(("batch", "expert"), None),
        P("expert", None, None),
        P("expert", None),
        P("expert", None, None),
        P("expert", None),
        P(),
        P(),
    )
    return jax.shard_map(shards, mesh=mesh, in_specs=in_specs, out_specs=out_specs, check_vma=False)
```

profile of v0, /device:TPU:0, one launch (start us, length us, event | category | flops | bytes accessed | tf_op | source)
XLA Modules:
  0.0 967.7 jit_solution(7064282413720540955)
XLA Ops:
  12.8 42.1 %all-reduce.10 = (bf16[768]{0:T(1024)(128)(2,1)S(1)}, bf16[768]{0:T(1024)(128)(2,1)S(1)}, bf16[768]{0:T(1024)(128)(2,1)S(1)}, bf16[768]{0:T(1024)(128)(2,1)S(1)}) all-reduce(bf16[768]{0:T(1024)(128)(2,1)S(1)} %dynamic-update-slice.1, bf16[768]{0:T(1024)(128)(2,1)S(1)} %dynamic-update-slice, ...), channel_id=1, replica_groups=mesh['batch'=4,'expert'=8] {'batch','expert'}, use_global_device_ids=true, to_apply=%add.1 | all-reduce | flops 3072 | bytes 12288
  64.3 9.6 all-gather.4.cloned.1.call-done
  88.7 73.2 %while.28 = (s32[]{:T(128)}, bf16[2,512,12,64]{1,3,2,0:T(8,128)(2,1)}, f32[2,12,512,1]{2,1,3,0:T(8,128)S(1)}, s32[2]{0:T(128)S(1)}, s32[1024]{0:T(1024)S(1)}, /*...) while((s32[]{:T(128)}, ...), condition=%wide.region_7.8_spmd.clone, body=%wide.region_4.7_spmd.clone.sunk | while | flops 1687677440 | bytes 190290176 | solution.py:116
  90.7 10.6 %fusion.152 = (f32[12,512]{1,0:T(8,128)S(1)}, f32[12,512,1024]{2,1,0:T(8,128)}) fusion(pred[512,1024]{1,0:T(8,128)(4,1)S(1)} %fusion.151, bf16[1024,12,64]{0,2,1:T(8,128)(2,1)S(1)} %get-tuple-element.506, bf16[1024,12,64]{0,2,1:T(8,128)(2,1)S(1)} %get-tuple-element.505, s32[]{:T(128)S(6)} %select_n.67), kind=kOutput, calls=%fused_computation.9.clone.1 | convolution fusion | flops 824174592 | bytes 28073988 | tf_op jit(solution)/shard_map/while/body/eval_jaxpr/qhd,khd->hqk/dot_general | solution.py:88
  101.3 12.3 %fusion.153 = f32[12,512]{1,0:T(8,128)S(1)} fusion(f32[12,512,1024]{2,1,0:T(8,128)} %get-tuple-element.461, f32[12,512]{1,0:T(8,128)S(1)} %get-tuple-element.462, pred[512,1024]{1,0:T(8,128)(4,1)S(1)} %fusion.151), kind=kLoop, calls=%fused_computation.10.clone.1 | loop fusion | flops 25159680 | bytes 25739264 | tf_op jit(solution)/shard_map/while/body/eval_jaxpr/reduce_sum | solution.py:100
  127.3 10.6 %fusion.152 = (f32[12,512]{1,0:T(8,128)S(1)}, f32[12,512,1024]{2,1,0:T(8,128)}) fusion(pred[512,1024]{1,0:T(8,128)(4,1)S(1)} %fusion.151, bf16[1024,12,64]{0,2,1:T(8,128)(2,1)S(1)} %get-tuple-element.506, bf16[1024,12,64]{0,2,1:T(8,128)(2,1)S(1)} %get-tuple-element.505, s32[]{:T(128)S(6)} %select_n.67), kind=kOutput, calls=%fused_computation.9.clone.1 | convolution fusion | flops 824174592 | bytes 28073988 | tf_op jit(solution)/shard_map/while/body/eval_jaxpr/qhd,khd->hqk/dot_general | solution.py:88
  137.8 12.3 %fusion.153 = f32[12,512]{1,0:T(8,128)S(1)} fusion(f32[12,512,1024]{2,1,0:T(8,128)} %get-tuple-element.461, f32[12,512]{1,0:T(8,128)S(1)} %get-tuple-element.462, pred[512,1024]{1,0:T(8,128)(4,1)S(1)} %fusion.151), kind=kLoop, calls=%fused_computation.10.clone.1 | loop fusion | flops 25159680 | bytes 25739264 | tf_op jit(solution)/shard_map/while/body/eval_jaxpr/reduce_sum | solution.py:100
  188.6 53.9 %all-to-all-done = bf16[8,192,768]{2,1,0:T(8,128)(2,1)} async-done(((bf16[8,192,768]{2,1,0:T(8,128)(2,1)}), bf16[8,192,768]{2,1,0:T(8,128)(2,1)}, u32[]{:S(2)}, u32[]{:S(2)}) %all-to-all-start) | async-done | bytes 2359328 | tf_op jit(solution)/shard_map/all_to_all | solution.py:137
  242.5 49.7 %multiply_convert_fusion.1 = (bf16[1536,3072]{1,0:T(8,128)(2,1)S(1)}, f32[1536,3072]{1,0:T(8,128)}, f32[1536,3072]{1,0:T(8,128)}) fusion(f32[3072]{0:T(1024)S(1)} %bitcast.191, bf16[1536,768]{1,0:T(8,128)(2,1)} %bitcast.12, bf16[1,768,3072]{2,1,0:T(8,128)(2,1)} %param.30), kind=kOutput, calls=%fused_computation.50 | convolution fusion | flops 7559184384 | bytes 54276096 | tf_op jit(solution)/shard_map/dot_general | solution.py:140
  304.6 109.4 %all-gather = bf16[32,24,8]{1,2,0:T(8,128)(2,1)S(1)} all-gather(bf16[1,24,8]{1,2,0:T(8,128)(2,1)S(1)} %bitcast.193), channel_id=1, replica_groups=mesh['batch'=4,'expert'=8] {'batch','expert'}, dimensions={0}, use_global_device_ids=true | all-gather | bytes 12672 | tf_op jit(solution)/shard_map/all_gather | solution.py:54
  437.7 55.2 %all_to_all.20 = bf16[8,192,768]{2,1,0:T(8,128)(2,1)S(1)} all-to-all(bf16[8,192,768]{2,1,0:T(8,128)(2,1)S(1)} %bitcast.166), channel_id=1, replica_groups=mesh['batch'=4,'expert'=8] {'expert'}, dimensions={0} | all-to-all | bytes 4718592 | tf_op jit(solution)/shard_map/all_to_all | solution.py:176
  492.9 24.4 %fusion.104 = (bf16[3072]{0:T(1024)(128)(2,1)}, bf16[1536,3072]{1,0:T(8,128)(2,1)}) fusion(f32[1536,3072]{1,0:T(8,128)} %get-tuple-element.333, bf16[1536,768]{1,0:T(8,128)(2,1)S(1)} %bitcast.163, bf16[1,3072,768]{2,1,0:T(8,128)(2,1)} %param.32, f32[1536,3072]{1,0:T(8,128)} %get-tuple-element.346, f32[3072]{0:T(1024)S(1)} %bitcast.192), kind=kOutput, calls=%fused_computation.175 | convolution fusion | flops 7323251712 | bytes 54282240 | tf_op jit(solution)/shard_map/rd,fd->rf/dot_general | solution.py:183
  517.3 11.1 %fusion.57 = bf16[1536,768]{1,0:T(8,128)(2,1)} fusion(bf16[1536,3072]{1,0:T(8,128)(2,1)} %get-tuple-element.351, bf16[1,768,3072]{2,1,0:T(8,128)(2,1)S(1)} %bitcast.196), kind=kOutput, calls=%fused_computation.95 | convolution fusion | flops 7248936960 | bytes 16515072 | tf_op jit(solution)/shard_map/rf,df->rd/dot_general | solution.py:196
  532.1 12.8 %fusion.50 = bf16[1,3072,768]{2,1,0:T(8,128)(2,1)} fusion(bf16[1536,3072]{1,0:T(8,128)(2,1)} %copy-done.68, bf16[1536,768]{1,0:T(8,128)(2,1)} %bitcast.164), kind=kOutput, calls=%fused_computation.89 | convolution fusion | flops 7250116608 | bytes 16515072 | tf_op jit(solution)/shard_map/rf,rd->fd/dot_general | solution.py:180
  544.9 12.3 %fusion.49 = bf16[1,768,3072]{2,1,0:T(8,128)(2,1)} fusion(bf16[1536,768]{1,0:T(8,128)(2,1)} %bitcast.12, bf16[1536,3072]{1,0:T(8,128)(2,1)} %get-tuple-element.351), kind=kOutput, calls=%fused_computation.88 | convolution fusion | flops 7250116608 | bytes 16515072 | tf_op jit(solution)/shard_map/rd,rf->df/dot_general | solution.py:189
  557.4 48.7 %psum.49 = f32[8]{0:T(128)S(1)} all-reduce(f32[8]{0:T(128)S(1)} %convert_reduce_fusion.1), channel_id=1, replica_groups=mesh['batch'=4,'expert'=8] {'batch','expert'}, use_global_device_ids=true, to_apply=%region_18.19 | all-reduce | flops 8 | bytes 64 | tf_op jit(solution)/shard_map/psum | solution.py:163
  633.0 179.0 %while.29 = (s32[]{:T(128)}, f32[1024,12,64]{0,2,1:T(8,128)}, f32[1024,12,64]{0,2,1:T(8,128)}, bf16[2,512,12,64]{1,3,2,0:T(8,128)(2,1)}, s32[2]{0:T(128)S(1)}, /...) while((s32[]{:T(128)}, f32[1024,12,64]{0,2,1:T(8,128)}, ...), condition=%wide.region_24.25_spmd.clone, body=%wide.region_22.24_spmd.clone.sunk | while | flops 4126796288 | bytes 225638736 | solution.py:259
  637.0 11.6 %fusion.163 = f32[12,512,1024]{2,1,0:T(8,128)} fusion(bf16[1024,12,64]{0,2,1:T(8,128)(2,1)S(1)} %get-tuple-element.551, bf16[1024,12,64]{0,2,1:T(8,128)(2,1)} %get-tuple-element.549, s32[]{:T(128)S(6)} %select_n.71), kind=kOutput, calls=%fused_computation.37.clone.1 | convolution fusion | flops 805306368 | bytes 27525124 | tf_op jit(solution)/shard_map/while/body/eval_jaxpr/qhd,khd->hqk/dot_general | solution.py:88
  648.6 14.5 %bitcast_add_fusion.5 = f32[1024,12,64]{0,2,1:T(8,128)} fusion(f32[1024,12,64]{0,2,1:T(8,128)} %get-tuple-element.530, f32[12,512,1024]{2,1,0:T(8,128)} %fusion.163, f32[12,512]{1,0:T(8,128)S(1)} %dynamic-slice_bitcast_fusion.2, pred[512,1024]{1,0:T(8,128)(4,1)S(1)} %fusion.164, pred[]{:T(512)S(6)} %compare.3, ...), kind=kOutput, calls=%fused_computation.28.clone.1 | convolution fusion | flops 832045056 | bytes 32800772 | tf_op jit(solution)/shard_map/while/body/eval_jaxpr/hqk,qhd->khd/dot_general | solution.py:250
  663.1 18.2 %multiply_reduce_fusion.8 = (f32[12,512]{1,0:T(8,128)S(1)}, f32[12,512,1024]{2,1,0:T(8,128)}) fusion(f32[12,512,1024]{2,1,0:T(8,128)} %fusion.163, f32[12,512]{1,0:T(8,128)S(1)} %dynamic-slice_bitcast_fusion.2, pred[512,1024]{1,0:T(8,128)(4,1)S(1)} %fusion.164, bf16[1024,12,64]{0,2,1:T(8,128)(2,1)} %get-tuple-element.554, ...), kind=kOutput, calls=%fused_computation.23.clone.1 | convolution fusion | flops 836757504 | bytes 53264388 | tf_op jit(solution)/shard_map/while/body/eval_jaxpr/qhd,khd->hqk/dot_general | solution.py:234
  681.4 23.2 %multiply_convert_fusion.3 = bf16[12,512,1024]{2,1,0:T(8,128)(2,1)} fusion(f32[12,512,1024]{2,1,0:T(8,128)} %get-tuple-element.474, f32[12,512,1024]{2,1,0:T(8,128)} %fusion.163, f32[12,512]{1,0:T(8,128)S(1)} %get-tuple-element.475, f32[12,512]{1,0:T(8,128)S(1)} %dynamic-slice_bitcast_fusion.2, pred[512,1024]{1,0:T(8,128)(4,1)S(1)} %fusion.164), kind=kLoop, calls=%fused_computation.22.clone.1 | loop fusion | flops 37748736 | bytes 63488000 | tf_op jit(solution)/shard_map/while/body/eval_jaxpr/convert_element_type | solution.py:238
  704.6 9.7 %bitcast_dynamic-update-slice_fusion.8 = bf16[2,512,12,64]{1,3,2,0:T(8,128)(2,1)} fusion(bf16[2,512,12,64]{1,3,2,0:T(8,128)(2,1)} %get-tuple-element.531, s32[]{:T(128)S(6)} %copy.123, bf16[12,512,1024]{2,1,0:T(8,128)(2,1)} %multiply_convert_fusion.3, bf16[1024,12,64]{0,2,1:T(8,128)(2,1)S(1)} %get-tuple-element.551), kind=kOutput, calls=%fused_computation.32.clone.1 | convolution fusion | flops 805699584 | bytes 15728644 | tf_op jit(solution)/shard_map/while/body/eval_jaxpr/hqk,khd->qhd/dot_general | solution.py:240
  726.7 11.4 %fusion.163 = f32[12,512,1024]{2,1,0:T(8,128)} fusion(bf16[1024,12,64]{0,2,1:T(8,128)(2,1)S(1)} %get-tuple-element.551, bf16[1024,12,64]{0,2,1:T(8,128)(2,1)} %get-tuple-element.549, s32[]{:T(128)S(6)} %select_n.71), kind=kOutput, calls=%fused_computation.37.clone.1 | convolution fusion | flops 805306368 | bytes 27525124 | tf_op jit(solution)/shard_map/while/body/eval_jaxpr/qhd,khd->hqk/dot_general | solution.py:88
  738.2 14.5 %bitcast_add_fusion.5 = f32[1024,12,64]{0,2,1:T(8,128)} fusion(f32[1024,12,64]{0,2,1:T(8,128)} %get-tuple-element.530, f32[12,512,1024]{2,1,0:T(8,128)} %fusion.163, f32[12,512]{1,0:T(8,128)S(1)} %dynamic-slice_bitcast_fusion.2, pred[512,1024]{1,0:T(8,128)(4,1)S(1)} %fusion.164, pred[]{:T(512)S(6)} %compare.3, ...), kind=kOutput, calls=%fused_computation.28.clone.1 | convolution fusion | flops 832045056 | bytes 32800772 | tf_op jit(solution)/shard_map/while/body/eval_jaxpr/hqk,qhd->khd/dot_general | solution.py:250
  752.7 18.3 %multiply_reduce_fusion.8 = (f32[12,512]{1,0:T(8,128)S(1)}, f32[12,512,1024]{2,1,0:T(8,128)}) fusion(f32[12,512,1024]{2,1,0:T(8,128)} %fusion.163, f32[12,512]{1,0:T(8,128)S(1)} %dynamic-slice_bitcast_fusion.2, pred[512,1024]{1,0:T(8,128)(4,1)S(1)} %fusion.164, bf16[1024,12,64]{0,2,1:T(8,128)(2,1)} %get-tuple-element.554, ...), kind=kOutput, calls=%fused_computation.23.clone.1 | convolution fusion | flops 836757504 | bytes 53264388 | tf_op jit(solution)/shard_map/while/body/eval_jaxpr/qhd,khd->hqk/dot_general | solution.py:234
  770.9 21.6 %multiply_convert_fusion.3 = bf16[12,512,1024]{2,1,0:T(8,128)(2,1)} fusion(f32[12,512,1024]{2,1,0:T(8,128)} %get-tuple-element.474, f32[12,512,1024]{2,1,0:T(8,128)} %fusion.163, f32[12,512]{1,0:T(8,128)S(1)} %get-tuple-element.475, f32[12,512]{1,0:T(8,128)S(1)} %dynamic-slice_bitcast_fusion.2, pred[512,1024]{1,0:T(8,128)(4,1)S(1)} %fusion.164), kind=kLoop, calls=%fused_computation.22.clone.1 | loop fusion | flops 37748736 | bytes 63488000 | tf_op jit(solution)/shard_map/while/body/eval_jaxpr/convert_element_type | solution.py:238
  792.5 9.7 bitcast_dynamic-update-slice_fusion.8
  802.2 9.6 bitcast_add_fusion.4
  832.1 10.4 %all-reduce.11 = (bf16[1,3072]{1,0:T(2,128)(2,1)S(1)}, bf16[1,768]{1,0:T(2,128)(2,1)S(1)}) all-reduce(bf16[1,3072]{1,0:T(2,128)(2,1)S(1)} %convert_element_type.171, bf16[1,768]{1,0:T(2,128)(2,1)S(1)} %convert_element_type.176), channel_id=1, replica_groups=mesh['batch'=4,'expert'=8] {'batch'}, use_global_device_ids=true, to_apply=%region_40.41 | all-reduce | flops 3840 | bytes 15360 | tf_op jit(solution)/shard_map/psum | solution.py:192
  845.3 9.3 fusion.103
  864.7 41.1 %all-reduce.9 = (f32[768]{0:T(1024)S(1)}, f32[768]{0:T(1024)S(1)}, f32[768]{0:T(1024)S(1)}, f32[768]{0:T(1024)S(1)}, f32[768,8]{0,1:T(8,128)S(1)}, /*index=5*/f32[8]{0:T(128)S(1)}, f32[3]{0:T(128)S(1)}) all-reduce(f32[768]{0:T(1024)S(1)} %get-tuple-element.269, ...), channel_id=4, replica_groups=mesh['batch'=4,'expert'=8] {'batch','expert'}, use_global_device_ids=true, to_apply=%region_30.31.clone | all-reduce | flops 9227 | bytes 73816
  932.4 27.3 %reduce-scatter.4.cloned.1.call-done = f32[24,2304]{1,0:T(8,128)} async-done(((f32[768,2304]{1,0:T(8,128)}), f32[24,2304]{1,0:T(8,128)}) %reduce-scatter.4.cloned.1.call-update) | async-done | bytes 221200 | tf_op jit(solution)/shard_map/reduce_scatter | solution.py:278
  (295 shorter events, 218.4 us)
Async XLA Ops:
  7.2 66.7 %all-gather.4.cloned.1.call-start = ((), (), s32[]{:S(2)}) async-start(), calls=%async_computation.6 | async-start | bytes 3649536 | tf_op jit(solution)/shard_map/all_gather | solution.py:48
  7.9 159.9 %all-gather.6.cloned.1.call-start = ((), (), s32[]{:S(2)}) async-start(), calls=%async_computation.7 | async-start | bytes 1216512 | tf_op jit(solution)/shard_map/all_gather | solution.py:49
  55.0 18.9 %copy-start.58 = (f32[768]{0:T(1024)}, f32[768]{0:T(1024)S(1)}, u32[]{:S(2)}) copy-start(f32[768]{0:T(1024)S(1)} %convert_element_type.146) | copy-start | bytes 9220
  55.1 18.8 %copy-start.37 = (f32[768]{0:T(1024)}, f32[768]{0:T(1024)S(1)}, u32[]{:S(2)}) copy-start(f32[768]{0:T(1024)S(1)} %convert_element_type.145) | copy-start | bytes 9220
  63.5 16.8 %copy-start.7 = (bf16[1024,768]{0,1:T(8,128)(2,1)}, bf16[1024,768]{0,1:T(8,128)(2,1)S(1)}, u32[]{:S(2)}) copy-start(bf16[1024,768]{0,1:T(8,128)(2,1)S(1)} %copy.79) | copy-start | bytes 4718596
  63.8 10.1 %copy-start.33 = (f32[1024]{0:T(1024)}, f32[1024]{0:T(1024)S(1)}, u32[]{:S(2)}) copy-start(f32[1024]{0:T(1024)S(1)} %broadcast_multiply_fusion.1) | copy-start | bytes 12292
  90.7 22.9 %copy-start.6 = (bf16[1024,12,64]{0,2,1:T(8,128)(2,1)S(1)}, bf16[1024,12,64]{0,2,1:T(8,128)(2,1)}, u32[]{:S(2)}) copy-start(bf16[1024,12,64]{0,2,1:T(8,128)(2,1)} %get-tuple-element.507) | copy-start | bytes 4718596 | tf_op jit(solution)/shard_map/while
  101.3 15.6 %copy-start = (f32[12,512,1024]{2,1,0:T(8,128)S(1)}, f32[12,512,1024]{2,1,0:T(8,128)}, u32[]{:S(2)}) copy-start(f32[12,512,1024]{2,1,0:T(8,128)} %get-tuple-element.461) | copy-start | bytes 75497472 | tf_op jit(solution)/shard_map/while
  127.3 22.9 %copy-start.6 = (bf16[1024,12,64]{0,2,1:T(8,128)(2,1)S(1)}, bf16[1024,12,64]{0,2,1:T(8,128)(2,1)}, u32[]{:S(2)}) copy-start(bf16[1024,12,64]{0,2,1:T(8,128)(2,1)} %get-tuple-element.507) | copy-start | bytes 4718596 | tf_op jit(solution)/shard_map/while
  137.8 15.4 %copy-start = (f32[12,512,1024]{2,1,0:T(8,128)S(1)}, f32[12,512,1024]{2,1,0:T(8,128)}, u32[]{:S(2)}) copy-start(f32[12,512,1024]{2,1,0:T(8,128)} %get-tuple-element.461) | copy-start | bytes 75497472 | tf_op jit(solution)/shard_map/while
  176.1 11.8 %copy-start.55 = (bf16[1,3072]{1,0:T(2,128)(2,1)S(1)}, bf16[1,3072]{1,0:T(2,128)(2,1)}, u32[]{:S(2)}) copy-start(bf16[1,3072]{1,0:T(2,128)(2,1)} %param.31) | copy-start | bytes 18436
  176.2 11.9 %copy-start.62 = (bf16[1,768]{1,0:T(2,128)(2,1)S(1)}, bf16[1,768]{1,0:T(2,128)(2,1)}, u32[]{:S(2)}) copy-start(bf16[1,768]{1,0:T(2,128)(2,1)} %param.33) | copy-start | bytes 4612
  183.2 59.3 %all-to-all-start = ((bf16[8,192,768]{2,1,0:T(8,128)(2,1)}), bf16[8,192,768]{2,1,0:T(8,128)(2,1)}, u32[]{:S(2)}, u32[]{:S(2)}) async-start(bf16[8,192,768]{2,1,0:T(8,128)(2,1)} %bitcast.165), calls=%async_computation | async-start | bytes 4718592 | tf_op jit(solution)/shard_map/all_to_all | solution.py:137
  242.5 49.7 %copy-start.57 = (f32[768]{0:T(1024)S(1)}, f32[768]{0:T(1024)}, u32[]{:S(2)}) copy-start(f32[768]{0:T(1024)} %convert_reduce_fusion.3) | copy-start | bytes 9220
  242.5 49.7 %copy-start.65 = (bf16[1,3072,768]{2,1,0:T(8,128)(2,1)S(1)}, bf16[1,3072,768]{2,1,0:T(8,128)(2,1)}, u32[]{:S(2)}) copy-start(bf16[1,3072,768]{2,1,0:T(8,128)(2,1)} %param.32) | copy-start | bytes 14155780
  300.8 116.2 %copy-start.54 = (s32[1024,1]{0,1:T(1,128)S(1)}, s32[1024,1]{0,1:T(1,128)}, u32[]{:S(2)}) copy-start(s32[1024,1]{0,1:T(1,128)} %compare_select_fusion) | copy-start | bytes 12292
  300.8 116.2 %copy-start.31 = (s32[1024,1]{0,1:T(1,128)S(1)}, s32[1024,1]{0,1:T(1,128)}, u32[]{:S(2)}) copy-start(s32[1024,1]{0,1:T(1,128)} %param.22) | copy-start | bytes 12292
  300.8 117.9 %all-to-all-start.1 = ((bf16[8,192,768]{2,1,0:T(8,128)(2,1)}), bf16[8,192,768]{2,1,0:T(8,128)(2,1)S(1)}, u32[]{:S(2)}, u32[]{:S(2)}) async-start(bf16[8,192,768]{2,1,0:T(8,128)(2,1)} %bitcast.170), calls=%async_computation.1 | async-start | bytes 4718592 | tf_op jit(solution)/shard_map/all_to_all | solution.py:148
  437.7 79.7 %slice-start = ((s8[4718592]{0:T(1024)(128)(4,1)}), s8[524288]{0:T(1024)(128)(4,1)S(1)}, s32[]{:S(2)}) async-start(s8[4718592]{0:T(1024)(128)(4,1)} %bitcast.195), calls=%async_computation.11 | async-start | bytes 1048576
  492.9 24.4 %copy-start.19 = (bf16[8,192,768]{2,1,0:T(8,128)(2,1)}, bf16[8,192,768]{2,1,0:T(8,128)(2,1)S(1)}, u32[]{:S(2)}) copy-start(bf16[8,192,768]{2,1,0:T(8,128)(2,1)S(1)} %all_to_all.20) | copy-start | bytes 7077892
  492.9 24.4 %slice-start.1 = ((s8[4718592]{0:T(1024)(128)(4,1)}), s8[4194304]{0:T(1024)(128)(4,1)S(1)}, s32[]{:S(2)}) async-start(s8[4718592]{0:T(1024)(128)(4,1)} %bitcast.195), calls=%async_computation.12 | async-start | bytes 8388608
  528.5 78.3 %all-to-all-start.3 = ((bf16[8,192,768]{2,1,0:T(8,128)(2,1)}), bf16[8,192,768]{2,1,0:T(8,128)(2,1)S(1)}, u32[]{:S(2)}, u32[]{:S(2)}) async-start(bf16[8,192,768]{2,1,0:T(8,128)(2,1)} %bitcast.169), calls=%async_computation.3 | async-start | bytes 4718592 | tf_op jit(solution)/shard_map/all_to_all | solution.py:199
  532.1 388.3 %all-reduce.15.cloned.1.call-start = ((), (), s32[]{:S(2)}) async-start(), calls=%async_computation.10 | async-start | bytes 18874368 | tf_op jit(solution)/shard_map/psum | solution.py:191
  557.2 375.1 %reduce-scatter.6.cloned.1.call-start = ((), (), s32[]{:S(2)}) async-start(), calls=%async_computation.9 | async-start | bytes 2433024 | tf_op jit(solution)/shard_map/reduce_scatter | solution.py:279
  627.5 332.1 %reduce-scatter.4.cloned.1.call-start = ((), (), s32[]{:S(2)}) async-start(), calls=%async_computation.8 | async-start | bytes 7299072 | tf_op jit(solution)/shard_map/reduce_scatter | solution.py:278
  637.0 11.6 %copy-start.18 = (bf16[1024,12,64]{0,2,1:T(8,128)(2,1)S(1)}, bf16[1024,12,64]{0,2,1:T(8,128)(2,1)}, u32[]{:S(2)}) copy-start(bf16[1024,12,64]{0,2,1:T(8,128)(2,1)} %get-tuple-element.553) | copy-start | bytes 4718596 | tf_op jit(solution)/shard_map/while
  704.5 9.7 %copy-start.5 = (bf16[1024,12,64]{0,2,1:T(8,128)(2,1)S(1)}, bf16[1024,12,64]{0,2,1:T(8,128)(2,1)}, u32[]{:S(2)}) copy-start(bf16[1024,12,64]{0,2,1:T(8,128)(2,1)} %get-tuple-element.549) | copy-start | bytes 4718596 | tf_op jit(solution)/shard_map/while
  726.7 11.4 %copy-start.18 = (bf16[1024,12,64]{0,2,1:T(8,128)(2,1)S(1)}, bf16[1024,12,64]{0,2,1:T(8,128)(2,1)}, u32[]{:S(2)}) copy-start(bf16[1024,12,64]{0,2,1:T(8,128)(2,1)} %get-tuple-element.553) | copy-start | bytes 4718596 | tf_op jit(solution)/shard_map/while
  792.5 9.7 copy-start.5
  829.9 13.9 %copy-start.22 = (bf16[1024,768]{0,1:T(8,128)(2,1)S(1)}, bf16[1024,768]{0,1:T(8,128)(2,1)}, u32[]{:S(2)}) copy-start(bf16[1024,768]{0,1:T(8,128)(2,1)} %get-tuple-element.340) | copy-start | bytes 4718596
  863.3 44.9 %copy-start.17 = (bf16[1024,768]{0,1:T(8,128)(2,1)S(1)}, bf16[1024,768]{0,1:T(8,128)(2,1)}, u32[]{:S(2)}) copy-start(bf16[1024,768]{0,1:T(8,128)(2,1)} %copy.87) | copy-start | bytes 4718596
  863.3 44.9 %copy-start.50 = (f32[1024]{0:T(1024)S(1)}, f32[1024]{0:T(1024)}, u32[]{:S(2)}) copy-start(f32[1024]{0:T(1024)} %copy-done.49) | copy-start | bytes 12292
  (51 other events, 208.0 us)
Sparse Core Ops, SparseCore 0:
  11.0 62.8 all-gather.3
  76.9 52.8 all-gather.5
  557.4 171.3 all-reduce.14
  734.5 99.7 reduce-scatter.5
  840.4 119.2 reduce-scatter.3
where the time goes:
time: 978 us; the launch traced here: 968 us
  matrix products  327 us (33%)
  blocking collectives  307 us (31%)
  other arithmetic  119 us (12%)
  waiting for transfers between devices  92.2 us (9%)
  local copies, waits for them, and re-layouts  86.6 us (9%)
  between operations  16.8 us (2%)
  starting transfers between devices  12.4 us (1%)
    all_gather x1, blocking collectives, shards(): lax.all_gather(router_weight, ('batch', 'expert'), axis=0, tiled=True)  109 us
    unnamed x2, blocking collectives  83.3 us
    all_to_all x1, blocking collectives, shards(): lax.all_to_all(to_experts(out_row_grad), 'expert', split_axis=0, concat_a...  55.2 us
    all_to_all x1, waiting for transfers between devices, shards(): lax.all_to_all(to_experts(second_low), 'expert', split_axis=0, concat_axi...  53.9 us
    dot_general x1, matrix products, shards(): jnp.dot(received, inner_weight[0], preferred_element_type=jnp.float32)  49.7 us
    psum x1, blocking collectives, shards(): lax.psum((local_counts, local_gates, local_squares), ('batch', 'expert'))  48.7 us
    convert_element_type x2, other arithmetic, backward_block(): score_grad = (attn_probs * (prob_grad - row_inner)).astype(jnp.bfloat16)  44.7 us
    dot_general x4, matrix products, block_scores(): jnp.einsum('qhd,khd->hqk', query_block, keys_all, preferred_element_type=...  44.2 us
  transfers between devices with their start and end apart: 8, of which 3 were waited for; matrix products, arithmetic and copies ran while one was open for 41% of the time, Pallas kernels for 0%

commit v1 on v0

v1 whole, which is shorter than its diff:
```python
import functools

import jax
import jax.numpy as jnp
import numpy as np
from jax import lax
from jax.experimental import pallas as pl
from jax.experimental.pallas import tpu as pltpu
from jax.sharding import PartitionSpec as P

HEADS = 12
HEAD_DIM = 64
PAIRS = HEADS // 2
WINDOW = 512
BLOCK = 256
EPSILON = 1e-05
LANES = 128
BF = jnp.bfloat16
F32 = jnp.float32
ANYWHERE = ("batch", "expert")

NT = (((1,), (1,)), ((), ()))
NN = (((1,), (0,)), ((), ()))


def mm(a, b, dims=NN):
    return lax.dot_general(a, b, dims, preferred_element_type=F32)


def call(body, name, grid, in_specs, out_specs, out_shape, scratch=(), flops=0, bytes_=0, prefetch=0, aliases=None):
    return pl.pallas_call(
        body,
        name=name,
        grid_spec=pltpu.PrefetchScalarGridSpec(
            num_scalar_prefetch=prefetch,
            grid=grid,
            in_specs=in_specs,
            out_specs=out_specs,
            scratch_shapes=list(scratch),
        ),
        out_shape=out_shape,
        input_output_aliases=aliases or {},
        cost_estimate=pl.CostEstimate(flops=int(flops), bytes_accessed=int(bytes_), transcendentals=0),
    )


def sds(shape, dtype):
    return jax.ShapeDtypeStruct(shape, dtype)


def full(shape):
    return pl.BlockSpec(shape, lambda *_: (0,) * len(shape))


def bits_of(size):
    return size.bit_length() - 1


def swap(value, axis, bit):
    size = lax.axis_size(axis)
    return lax.ppermute(value, axis, [(i, i ^ (1 << bit)) for i in range(size)])


def my_bit(axis, bit):
    return (lax.axis_index(axis) >> bit) & 1


def gather_rows(shard):
    nb, ne = lax.axis_size("batch"), lax.axis_size("expert")
    value = shard
    placed = []
    order = [("expert", b) for b in reversed(range(bits_of(ne)))] + [("batch", b) for b in reversed(range(bits_of(nb)))]
    for axis, bit in order:
        weight = bit + (bits_of(ne) if axis == "batch" else 0)
        spot = sum(1 for w in placed if w > weight)
        placed.append(weight)
        other = swap(value, axis, bit)
        mine_high = my_bit(axis, bit) == 1
        low = jnp.where(mine_high, other, value)
        high = jnp.where(mine_high, value, other)
        value = jnp.stack([low, high], axis=spot)
    return value.reshape(nb * ne * shard.shape[0], shard.shape[1])


def scatter_rows(parts, rows_each):
    nb, ne = lax.axis_size("batch"), lax.axis_size("expert")
    ny = nb // 2
    core = my_bit("batch", 0)

    def half(which):
        return jnp.concatenate(
            [
                lax.dynamic_index_in_dim(p.reshape(ny, 2, ne, rows_each, p.shape[1]), which, 1, keepdims=False).astype(BF)
                for p in parts
            ],
            axis=-1,
        )

    got = swap(half(1 - core), "batch", 0)
    total = (half(core).astype(F32) + got.astype(F32)).astype(BF)
    total = jnp.swapaxes(total, 0, 1)
    pieces = lax.all_to_all(total, "expert", split_axis=0, concat_axis=0, tiled=True)
    value = jnp.sum(pieces.astype(F32), axis=0)
    for bit in reversed(range(1, bits_of(nb))):
        here = my_bit("batch", bit)
        value = value.reshape((2, value.shape[0] // 2) + value.shape[1:])
        out = lax.dynamic_index_in_dim(value, 1 - here, 0, keepdims=False)
        value = lax.dynamic_index_in_dim(value, here, 0, keepdims=False) + swap(out, "batch", bit)
    return value[0]


def sum_all(value):
    for axis in ("expert", "batch"):
        for bit in range(bits_of(lax.axis_size(axis))):
            value = value + swap(value, axis, bit)
    return value


def prep_body(lengths_ref, routes_col, routes_row, tgt_row, start_row, counts, *, capacity):
    rows = routes_row.shape[1]
    at = lax.broadcasted_iota(jnp.int32, (1, rows), 1)
    start = jnp.zeros((1, rows), jnp.int32)
    off = jnp.int32(0)
    for s in range(lengths_ref.shape[1]):
        start = jnp.where(at >= off, off, start)
        off = off + lengths_ref[0, s]
    start_row[...] = start
    hot = routes_row[...] == lax.broadcasted_iota(jnp.int32, (LANES, rows), 0)
    hot_low = jnp.where(hot, 1.0, 0.0).astype(BF)
    before = lax.broadcasted_iota(jnp.int32, (rows, rows), 0) < lax.broadcasted_iota(jnp.int32, (rows, rows), 1)
    ranks = mm(hot_low, jnp.where(before, 1.0, 0.0).astype(BF))
    rank = jnp.sum(jnp.where(hot, ranks, 0.0), axis=0, keepdims=True)
    tgt_row[...] = routes_row[...] * capacity + rank.astype(jnp.int32)
    hot_col = routes_col[...] == lax.broadcasted_iota(jnp.int32, (rows, LANES), 1)
    counts[...] = jnp.sum(jnp.where(hot_col, 1.0, 0.0), axis=0, keepdims=True)


def prepare(lengths, routes, capacity):
    rows = routes.shape[0]
    return call(
        functools.partial(prep_body, capacity=capacity),
        "prep",
        (1,),
        [pl.BlockSpec(memory_space=pltpu.SMEM), full((rows, 1)), full((1, rows))],
        [full((1, rows)), full((1, rows)), full((1, LANES))],
        [sds((1, rows), jnp.int32), sds((1, rows), jnp.int32), sds((1, LANES), F32)],
        flops=2 * rows * rows * LANES,
        bytes_=rows * 1024,
    )(lengths, routes, routes.reshape(1, rows))


def dispatch_body(slots, tgt, x, out):
    hot = jnp.where(slots[...] == tgt[...], 1.0, 0.0).astype(BF)
    out[0] = mm(hot, x[...]).astype(BF)


def dispatch(slots_col, tgt_row, x):
    rows, width = x.shape
    half = slots_col.shape[0] // 2
    tile = BLOCK
    per = half // tile
    return call(
        dispatch_body,
        "dispatch",
        (2, per),
        [
            pl.BlockSpec((tile, 1), lambda c, t: (c * per + t, 0)),
            full((1, rows)),
            full((rows, width)),
        ],
        pl.BlockSpec((1, tile, width), lambda c, t: (c, t, 0)),
        sds((2, half, width), BF),
        flops=4 * half * rows * width,
        bytes_=rows * width * 5,
    )(slots_col, tgt_row, x)


def normalise(v):
    centre = v - jnp.mean(v, axis=-1, keepdims=True)
    spread = jnp.mean(centre * centre, axis=-1, keepdims=True)
    scale = lax.rsqrt(spread + EPSILON)
    return centre * scale, scale


def first_body(tokens, gains, mixer, mixed, normed_t, *, gain_at):
    hat, _ = normalise(tokens[...].astype(F32))
    normed = hat * gains[gain_at : gain_at + 1, :] + gains[gain_at + 1 : gain_at + 2, :]
    low = normed.astype(BF)
    normed_t[...] = low.T
    mixed[...] = mm(low, mixer[...]).astype(BF)


def first_stage(tokens, gains, gathered, gain_at):
    rows, width = tokens.shape
    wide = 3 * width
    return call(
        functools.partial(first_body, gain_at=gain_at),
        "first",
        (rows // BLOCK,),
        [
            pl.BlockSpec((BLOCK, width), lambda i: (i, 0)),
            full((LANES, width)),
            pl.BlockSpec((width, wide), lambda i: (0, 0)),
        ],
        [pl.BlockSpec((BLOCK, wide), lambda i: (i, 0)), pl.BlockSpec((width, BLOCK), lambda i: (0, i))],
        [sds((rows, wide), BF), sds((width, rows), BF)],
        flops=2 * rows * width * wide,
        bytes_=2 * (rows * (2 * width + wide) + width * wide),
    )(tokens, gains, gathered)


def fill_bias(bias, start):
    rows = bias.shape[0]
    for q in range(rows // BLOCK):
        k0 = max(0, (q + 1) * BLOCK - WINDOW - BLOCK)
        n = (q + 1) * BLOCK - k0
        key = k0 + lax.broadcasted_iota(jnp.int32, (n, BLOCK), 0)
        query = q * BLOCK + lax.broadcasted_iota(jnp.int32, (n, BLOCK), 1)
        seen = (key <= query) & (key >= start[:, q * BLOCK : (q + 1) * BLOCK])
        bias[k0 : k0 + n, q * BLOCK : (q + 1) * BLOCK] = jnp.where(seen, 0.0, -1e30)


def head_of(value, h):
    lane = lax.broadcasted_iota(jnp.int32, value.shape, 1)
    return jnp.where((lane >= HEAD_DIM * h) & (lane < HEAD_DIM * (h + 1)), value, jnp.zeros_like(value))


def attend_body(start, q, k, v, att, att_t, lse, bias, v_t):
    rows = q.shape[0]

    @pl.when(pl.program_id(0) == 0)
    def _():
        fill_bias(bias, start[...])

    v_t[...] = v[...].T
    for i in range(rows // BLOCK):
        k0 = max(0, (i + 1) * BLOCK - WINDOW - BLOCK)
        k1 = (i + 1) * BLOCK
        here = slice(i * BLOCK, k1)
        scaled = q[here, :] * jnp.asarray(HEAD_DIM**-0.5, BF)
        for h in range(2):
            s = mm(k[k0:k1, :], head_of(scaled, h), NT) + bias[k0:k1, here]
            top = jnp.max(s, axis=0, keepdims=True)
            e = jnp.exp(s - top)
            total = jnp.sum(e, axis=0, keepdims=True)
            o = mm(v_t[HEAD_DIM * h : HEAD_DIM * (h + 1), k0:k1], e.astype(BF)) / total
            att_t[HEAD_DIM * h : HEAD_DIM * (h + 1), here] = o.astype(BF)
            lse[0, h : h + 1, here] = top + jnp.log(total)
    att[...] = att_t[...].T


def attend(mixed, start_row):
    rows = mixed.shape[0]
    width = mixed.shape[1] // 3
    return call(
        attend_body,
        "attend",
        (PAIRS,),
        [
            full((1, rows)),
            pl.BlockSpec((rows, LANES), lambda p: (0, p)),
            pl.BlockSpec((rows, LANES), lambda p: (0, PAIRS + p)),
            pl.BlockSpec((rows, LANES), lambda p: (0, 2 * PAIRS + p)),
        ],
        [
            pl.BlockSpec((rows, LANES), lambda p: (0, p)),
            pl.BlockSpec((LANES, rows), lambda p: (p, 0)),
            pl.BlockSpec((1, 8, rows), lambda p: (p, 0, 0)),
        ],
        [sds((rows, width), BF), sds((width, rows), BF), sds((PAIRS, 8, rows), F32)],
        [pltpu.VMEM((rows, rows), F32), pltpu.VMEM((LANES, rows), BF)],
        flops=8 * HEADS * rows * rows * HEAD_DIM,
        bytes_=2 * rows * width * 5,
    )(start_row, mixed, mixed, mixed)


def attend_back_body(start, q, k, v, g, lse, normed_t, dq, dk, dv, wq, wk, wv, bias, k_t, dq_t, dk_acc, dv_acc):
    rows = q.shape[0]

    @pl.when(pl.program_id(0) == 0)
    def _():
        fill_bias(bias, start[...])

    k_t[...] = k[...].T
    dk_acc[...] = jnp.zeros_like(dk_acc)
    dv_acc[...] = jnp.zeros_like(dv_acc)
    for i in range(rows // BLOCK):
        k0 = max(0, (i + 1) * BLOCK - WINDOW - BLOCK)
        k1 = (i + 1) * BLOCK
        here = slice(i * BLOCK, k1)
        scaled = q[here, :] * jnp.asarray(HEAD_DIM**-0.5, BF)
        g_here = g[here, :]
        for h in range(2):
            q_h = head_of(scaled, h)
            g_h = head_of(g_here, h)
            s = mm(k[k0:k1, :], q_h, NT) + bias[k0:k1, here]
            p = jnp.exp(s - lse[0, h : h + 1, here])
            dp = mm(v[k0:k1, :], g_h, NT)
            inner = jnp.sum(p * dp, axis=0, keepdims=True)
            ds = (p * (dp - inner)).astype(BF)
            dv_acc[k0:k1, :] += mm(p.astype(BF), g_h)
            dk_acc[k0:k1, :] += mm(ds, q_h)
            dq_t[HEAD_DIM * h : HEAD_DIM * (h + 1), here] = mm(k_t[HEAD_DIM * h : HEAD_DIM * (h + 1), k0:k1], ds)
    dq[...] = (dq_t[...].T * HEAD_DIM**-0.5).astype(BF)
    dk[...] = dk_acc[...].astype(BF)
    dv[...] = dv_acc[...].astype(BF)
    wq[...] = mm(normed_t[...], dq[...]).astype(BF)
    wk[...] = mm(normed_t[...], dk[...]).astype(BF)
    wv[...] = mm(normed_t[...], dv[...]).astype(BF)


def attend_back(mixed, attended_grad, lse, start_row, normed_t):
    rows, width = attended_grad.shape
    column = pl.BlockSpec((rows, LANES), lambda p: (0, p))
    return call(
        attend_back_body,
        "attend_back",
        (PAIRS,),
        [
            full((1, rows)),
            column,
            pl.BlockSpec((rows, LANES), lambda p: (0, PAIRS + p)),
            pl.BlockSpec((rows, LANES), lambda p: (0, 2 * PAIRS + p)),
            column,
            pl.BlockSpec((1, 8, rows), lambda p: (p, 0, 0)),
            full((width, rows)),
        ],
        [column] * 3 + [pl.BlockSpec((width, LANES), lambda p: (0, p))] * 3,
        [sds((rows, width), BF)] * 3 + [sds((width, width), BF)] * 3,
        [
            pltpu.VMEM((rows, rows), F32),
            pltpu.VMEM((LANES, rows), BF),
            pltpu.VMEM((LANES, rows), F32),
            pltpu.VMEM((rows, LANES), F32),
            pltpu.VMEM((rows, LANES), F32),
        ],
        flops=20 * HEADS * rows * rows * HEAD_DIM,
        bytes_=2 * rows * width * 10,
    )(start_row, mixed, mixed, mixed, attended_grad, lse, normed_t)


def second_body(att, w, tokens, gains, router, routes, stream, low, gates, sums, *, gain_at):
    attn = mm(att[...], w[...])
    total = tokens[...].astype(F32) + attn
    stream[...] = total
    hat, _ = normalise(total)
    normed = (hat * gains[gain_at : gain_at + 1, :] + gains[gain_at + 1 : gain_at + 2, :]).astype(BF)
    low[...] = normed
    logits = mm(normed, router[...])
    hot = routes[...] == lax.broadcasted_iota(jnp.int32, logits.shape, 1)
    gate = jax.nn.sigmoid(jnp.sum(jnp.where(hot, logits, 0.0), axis=1, keepdims=True))
    gates[...] = gate

    @pl.when(pl.program_id(0) == 0)
    def _():
        sums[...] = jnp.zeros_like(sums)

    row = lax.broadcasted_iota(jnp.int32, sums.shape, 0)
    by_expert = jnp.sum(jnp.where(hot, gate, 0.0), axis=0, keepdims=True)
    squares = jnp.sum(attn * attn)
    sums[...] += jnp.where(row == 0, by_expert, jnp.where(row == 1, squares, 0.0))


def second_stage(att, gathered, tokens, gains, routes, gain_at):
    rows, width = tokens.shape
    block = pl.BlockSpec((BLOCK, width), lambda i: (i, 0))
    thin = pl.BlockSpec((BLOCK, 1), lambda i: (i, 0))
    return call(
        functools.partial(second_body, gain_at=gain_at),
        "second",
        (rows // BLOCK,),
        [
            block,
            pl.BlockSpec((width, width), lambda i: (0, 3)),
            block,
            full((LANES, width)),
            pl.BlockSpec((width, LANES), lambda i: (0, 4 * width // LANES)),
            thin,
        ],
        [block, block, thin, full((8, LANES))],
        [sds((rows, width), F32), sds((rows, width), BF), sds((rows, 1), F32), sds((8, LANES), F32)],
        flops=2 * rows * width * width,
        bytes_=rows * width * 10 + width * width * 2,
    )(att, gathered, tokens, gains, gathered, routes)


def expert_body(
    bal, x, c, w1t, w2, w2t, w1, b1, b2, rw, act_t, pre_t, g_out, x_t, out, in_grad, b1_grad, rows_out,
    g, gate, out_acc, in_acc,
):
    step = pl.program_id(0)

    @pl.when(step == 0)
    def _():
        logits = jnp.sum(x[...].astype(F32) * rw[...], axis=1, keepdims=True)
        gate[...] = jax.nn.sigmoid(logits)
        g[...] = (gate[...] * c[...].astype(F32)).astype(BF)
        out_acc[...] = jnp.zeros_like(out_acc)
        in_acc[...] = jnp.zeros_like(in_acc)

    pre = mm(w1t[...], x[...], NT) + b1[...]
    cdf = 0.5 * (1.0 + lax.erf(pre * (0.5**0.5)))
    act = (pre * cdf).astype(BF)
    slope = cdf + pre * jnp.exp(-0.5 * pre * pre) * ((2.0 * np.pi) ** -0.5)
    act_t[...] = act
    out_acc[...] += mm(w2t[...], act)
    back = (mm(w2[...], g[...], NT) * slope).astype(BF)
    pre_t[...] = back
    in_acc[...] += mm(w1[...], back)
    b1_grad[...] = jnp.sum(back.astype(F32), axis=1, keepdims=True)

    @pl.when(step == pl.num_programs(0) - 1)
    def _():
        result = (out_acc[...].T + b2[...]).astype(BF)
        out[...] = result
        gate_grad = jnp.sum(c[...].astype(F32) * result.astype(F32), axis=1, keepdims=True) + bal[0, 0]
        logit_grad = gate_grad * gate[...] * (1.0 - gate[...])
        in_grad[...] = (in_acc[...].T + logit_grad * rw[...]).astype(BF)
        g_out[...] = g[...]
        x_t[...] = x[...].T
        row = lax.broadcasted_iota(jnp.int32, rows_out.shape, 0)
        router_part = jnp.sum(x[...].astype(F32) * logit_grad, axis=0, keepdims=True)
        bias_part = jnp.sum(g[...].astype(F32), axis=0, keepdims=True)
        rows_out[...] = jnp.where(row == 0, router_part, jnp.where(row == 1, bias_part, 0.0))


def expert_stage(bal, x, c, w1t, w2, w2t, w1, b1, b2, rw):
    rows, width = x.shape
    wide = w1.shape[1]
    tile = BLOCK
    across = pl.BlockSpec((tile, width), lambda f: (f, 0))
    down = pl.BlockSpec((width, tile), lambda f: (0, f))
    whole = full((rows, width))
    return call(
        expert_body,
        "expert",
        (wide // tile,),
        [
            pl.BlockSpec(memory_space=pltpu.SMEM),
            whole,
            whole,
            across,
            across,
            down,
            down,
            pl.BlockSpec((tile, 1), lambda f: (f, 0)),
            full((1, width)),
            full((1, width)),
        ],
        [
            pl.BlockSpec((tile, rows), lambda f: (f, 0)),
            pl.BlockSpec((tile, rows), lambda f: (f, 0)),
            whole,
            full((width, rows)),
            whole,
            whole,
            pl.BlockSpec((tile, 1), lambda f: (f, 0)),
            full((8, width)),
        ],
        [
            sds((wide, rows), BF),
            sds((wide, rows), BF),
            sds((rows, width), BF),
            sds((width, rows), BF),
            sds((rows, width), BF),
            sds((rows, width), BF),
            sds((wide, 1), F32),
            sds((8, width), F32),
        ],
        [
            pltpu.VMEM((rows, width), BF),
            pltpu.VMEM((rows, 1), F32),
            pltpu.VMEM((width, rows), F32),
            pltpu.VMEM((width, rows), F32),
        ],
        flops=8 * rows * width * wide,
        bytes_=2 * (4 * width * wide + 2 * wide * rows + 6 * rows * width),
    )(bal, x, c, w1t, w2, w2t, w1, b1, b2, rw)


def outer_grad_body(core, a0, a1, g0, g1, *rest):
    total = mm(a0[...], g0[...]) + mm(a1[...], g1[...])
    if len(rest) == 2:
        total = total + rest[0][...].astype(F32)
    rest[-1][...] = total.astype(BF)


def inner_grad_body(core, a0, a1, x0, x1, *rest):
    total = mm(x0[...], a0[...], NT) + mm(x1[...], a1[...], NT)
    if len(rest) == 2:
        total = total + rest[0][...].astype(F32)
    rest[-1][...] = total.astype(BF)


def weight_grad(which, outer, acts, others, width, wide, add=None):
    tile = 512
    steps = wide // 2 // tile
    rows = acts[0].shape[1]
    a_spec = pl.BlockSpec((tile, rows), lambda f, s: (s[0] * steps + f, 0))
    if outer:
        o_spec = pl.BlockSpec((tile, width), lambda f, s: (f, 0))
        shape = (wide // 2, width)
    else:
        o_spec = pl.BlockSpec((width, tile), lambda f, s: (0, f))
        shape = (width, wide // 2)
    specs = [a_spec, a_spec, full(others[0].shape), full(others[1].shape)]
    operands = [which, acts[0], acts[1], others[0], others[1]]
    if add is not None:
        specs.append(o_spec)
        operands.append(add)
    return call(
        outer_grad_body if outer else inner_grad_body,
        "weight_grad",
        (steps,),
        specs,
        o_spec,
        sds(shape, BF),
        flops=2 * rows * width * wide,
        bytes_=2 * (wide * rows + 2 * rows * width + width * wide),
        prefetch=1,
    )(*operands)


def own_half_body(which, a, b, out, low):
    total = a[...].astype(F32) + b[...].astype(F32)
    low[...] = total.astype(BF)
    out[0] = total.astype(BF).astype(F32)


def other_half_body(which, held, a, out):
    out[0] = a[...].astype(F32)


def half_specs(outer, shape):
    steps = 3
    if outer:
        block = (shape[0] // steps, shape[1])
        small = pl.BlockSpec(block, lambda i, s: (i, 0))
        large = pl.BlockSpec((1,) + block, lambda i, s: (0, s[0] * steps + i, 0))
        whole = (1, 2 * shape[0], shape[1])
    else:
        block = (shape[0], shape[1] // steps)
        small = pl.BlockSpec(block, lambda i, s: (0, i))
        large = pl.BlockSpec((1,) + block, lambda i, s: (0, 0, s[0] * steps + i))
        whole = (1, shape[0], 2 * shape[1])
    return steps, small, large, whole


def own_half(which, outer, a, b):
    steps, small, large, whole = half_specs(outer, a.shape)
    return call(
        own_half_body, "own_half", (steps,), [small, small], [large, small],
        [sds(whole, F32), sds(a.shape, BF)], bytes_=a.size * 10, flops=a.size, prefetch=1,
    )(which, a, b)


def other_half(which, outer, held, a):
    steps, small, large, whole = half_specs(outer, a.shape)
    return call(
        other_half_body, "other_half", (steps,), [pl.BlockSpec(memory_space=pl.ANY), small], large,
        sds(whole, F32), bytes_=a.size * 6, flops=a.size, prefetch=1, aliases={1: 0},
    )(which, held, a)


def layer_back(hat, scale, gain, grad):
    scaled = grad * gain
    return scale * (
        scaled - jnp.mean(scaled, axis=-1, keepdims=True) - hat * jnp.mean(scaled * hat, axis=-1, keepdims=True)
    )


def return_body(slots, tgt, r0, r1, stream, cot, gains, att_t, w, stream_grad, back, sums, w_grad, w_acc, *, gain_at):
    step = pl.program_id(0)

    @pl.when(step == 0)
    def _():
        sums[...] = jnp.zeros_like(sums)
        w_acc[...] = jnp.zeros_like(w_acc)

    grad = mm(jnp.where(tgt[...] == slots[0:1, :], 1.0, 0.0).astype(BF), r0[...])
    grad += mm(jnp.where(tgt[...] == slots[1:2, :], 1.0, 0.0).astype(BF), r1[...])
    hat, scale = normalise(stream[...])
    total = cot[...].astype(F32) + layer_back(hat, scale, gains[gain_at : gain_at + 1, :], grad)
    stream_grad[...] = total
    low = total.astype(BF)
    back[...] = mm(low, w[...], NT).astype(BF)
    w_acc[...] += mm(att_t[...], low)
    row = lax.broadcasted_iota(jnp.int32, sums.shape, 0)
    sums[...] += jnp.where(
        row == 0,
        jnp.sum(grad * hat, axis=0, keepdims=True),
        jnp.where(row == 1, jnp.sum(grad, axis=0, keepdims=True), 0.0),
    )

    @pl.when(step == pl.num_programs(0) - 1)
    def _():
        w_grad[...] = w_acc[...].astype(BF)


def return_stage(slots_row, tgt_col, r0, r1, stream, cot, gains, att_t, gathered, gain_at):
    rows, width = stream.shape
    block = pl.BlockSpec((BLOCK, width), lambda i: (i, 0))
    return call(
        functools.partial(return_body, gain_at=gain_at),
        "return",
        (rows // BLOCK,),
        [
            full(slots_row.shape),
            pl.BlockSpec((BLOCK, 1), lambda i: (i, 0)),
            full(r0.shape),
            full(r1.shape),
            block,
            block,
            full((LANES, width)),
            pl.BlockSpec((width, BLOCK), lambda i: (0, i)),
            pl.BlockSpec((width, width), lambda i: (0, 3)),
        ],
        [block, block, full((8, width)), full((width, width))],
        [sds((rows, width), F32), sds((rows, width), BF), sds((8, width), F32), sds((width, width), BF)],
        [pltpu.VMEM((width, width), F32)],
        flops=2 * rows * width * (2 * r0.shape[0] + 2 * width),
        bytes_=rows * width * 16 + 4 * width * width,
    )(slots_row, tgt_col, r0, r1, stream, cot, gains, att_t, gathered)


def last_body(dq, dk, dv, wq, wk, wv, tokens, stream_grad, gains, out, sums, *, gain_at):
    @pl.when(pl.program_id(0) == 0)
    def _():
        sums[...] = jnp.zeros_like(sums)

    grad = mm(dq[...], wq[...], NT) + mm(dk[...], wk[...], NT) + mm(dv[...], wv[...], NT)
    hat, scale = normalise(tokens[...].astype(F32))
    out[...] = stream_grad[...] + layer_back(hat, scale, gains[gain_at : gain_at + 1, :], grad)
    row = lax.broadcasted_iota(jnp.int32, sums.shape, 0)
    sums[...] += jnp.where(
        row == 0,
        jnp.sum(grad * hat, axis=0, keepdims=True),
        jnp.where(row == 1, jnp.sum(grad, axis=0, keepdims=True), 0.0),
    )


def last_stage(dq, dk, dv, gathered, tokens, stream_grad, gains, gain_at):
    rows, width = tokens.shape
    block = pl.BlockSpec((BLOCK, width), lambda i: (i, 0))
    weights = [pl.BlockSpec((width, width), functools.partial(lambda j, i: (0, j), j)) for j in range(3)]
    return call(
        functools.partial(last_body, gain_at=gain_at),
        "last",
        (rows // BLOCK,),
        [block] * 3 + weights + [block, block, full((LANES, width))],
        [block, full((8, width))],
        [sds((rows, width), F32), sds((8, width), F32)],
        flops=6 * rows * width * width,
        bytes_=rows * width * 16 + 6 * width * width,
    )(dq, dk, dv, gathered, gathered, gathered, tokens, stream_grad, gains)


def result_body(slots, tgt, r0, r1, stream, gates, out, sums):
    @pl.when(pl.program_id(0) == 0)
    def _():
        sums[...] = jnp.zeros_like(sums)

    picked = mm(jnp.where(tgt[...] == slots[0:1, :], 1.0, 0.0).astype(BF), r0[...])
    picked += mm(jnp.where(tgt[...] == slots[1:2, :], 1.0, 0.0).astype(BF), r1[...])
    moe = gates[...] * picked
    total = stream[...] + moe
    out[...] = total.astype(BF)
    row = lax.broadcasted_iota(jnp.int32, sums.shape, 0)
    sums[...] += jnp.where(row == 0, jnp.sum(total * total), jnp.where(row == 1, jnp.sum(moe * moe), 0.0))


def result_stage(slots_row, tgt_col, r0, r1, stream, gates):
    rows, width = stream.shape
    block = pl.BlockSpec((BLOCK, width), lambda i: (i, 0))
    thin = pl.BlockSpec((BLOCK, 1), lambda i: (i, 0))
    return call(
        result_body,
        "result",
        (rows // BLOCK,),
        [full(slots_row.shape), thin, full(r0.shape), full(r1.shape), block, thin],
        [block, full((8, LANES))],
        [sds((rows, width), BF), sds((8, LANES), F32)],
        flops=4 * rows * width * r0.shape[0],
        bytes_=rows * width * 10,
    )(slots_row, tgt_col, r0, r1, stream, gates)


def shards(
    tokens, cotangent, lengths, routes, mixer_weight, output_weight, first_gain, first_shift, second_gain,
    second_shift, router_weight, inner_weight, inner_bias, outer_weight, outer_bias,
):
    rows, width = tokens.shape
    shard_rows = mixer_weight.shape[0]
    experts = router_weight.shape[1]
    wide = inner_weight.shape[2]
    devices = lax.axis_size(ANYWHERE)
    capacity = 3 * rows // (2 * experts)
    half_cap = capacity // 2
    half = experts * half_cap
    total_tokens = rows * devices
    average = total_tokens / experts
    gain_one_at, gain_two_at, counts_at = experts, experts + 2, experts + 4

    slot_ids = np.arange(experts * capacity, dtype=np.int32).reshape(experts, 2, half_cap).swapaxes(0, 1).reshape(2, half)
    slots_row = jnp.asarray(slot_ids)
    slots_col = jnp.asarray(slot_ids.reshape(2 * half, 1))

    tgt_row, start_row, counts_here = prepare(lengths, routes, capacity)
    tgt_col = tgt_row.reshape(rows, 1)

    first_row = (lax.broadcasted_iota(jnp.int32, (shard_rows, 1), 0) == 0).astype(F32)
    small = jnp.concatenate(
        [
            router_weight,
            first_gain[:, None],
            first_shift[:, None],
            second_gain[:, None],
            second_shift[:, None],
            (first_row * counts_here[:, :experts]).astype(BF),
            jnp.zeros((shard_rows, LANES - 2 * experts - 4), BF),
        ],
        axis=1,
    )
    gathered = gather_rows(jnp.concatenate([mixer_weight, output_weight, small], axis=1))
    small_t = gathered[:, 4 * width :].T.astype(F32)
    counts = jnp.sum(small_t[counts_at : counts_at + experts], axis=1)
    expert_here = lax.axis_index("expert")
    balance_terms = (counts - average) / (average * total_tokens)
    bal = lax.dynamic_slice_in_dim(balance_terms, expert_here, 1).reshape(1, 1)
    rw = lax.dynamic_slice_in_dim(small_t, expert_here, 1, axis=0)

    def exchange(value):
        shaped = value.reshape(experts, half_cap, width)
        return lax.all_to_all(shaped, "expert", split_axis=0, concat_axis=0, tiled=True).reshape(half, width)

    mixed, normed_t = first_stage(tokens, small_t, gathered, gain_one_at)
    cot_placed = dispatch(slots_col, tgt_row, cotangent)
    cot_in, mixed = lax.optimization_barrier((cot_placed, mixed))
    cots = [exchange(cot_in[0]), exchange(cot_in[1])]
    att, att_t, lse = attend(mixed, start_row)
    stream, second_low, gates, second_sums = second_stage(att, gathered, tokens, small_t, routes, gain_two_at)
    placed = dispatch(slots_col, tgt_row, second_low)

    w1, w2 = inner_weight[0], outer_weight[0]
    w1t, w2t = w1.T, w2.T
    b1 = inner_bias.reshape(wide, 1).astype(F32)
    b2 = outer_bias.astype(F32)
    x0 = exchange(placed[0])
    second_half, x0 = lax.optimization_barrier((placed[1], x0))
    x1 = exchange(second_half)
    e0 = expert_stage(bal, x0, cots[0], w1t, w2, w2t, w1, b1, b2, rw)
    in0 = exchange(e0[5])
    e1 = expert_stage(bal, x1, cots[1], w1t, w2, w2t, w1, b1, b2, rw)
    in1 = exchange(e1[5])

    core = my_bit("batch", 0).reshape(1).astype(jnp.int32)
    nb_bits = bits_of(lax.axis_size("batch"))

    def over_batch(outer, acts, others):
        sent = swap(weight_grad(1 - core, outer, acts, others, width, wide), "batch", 0)
        mine = weight_grad(core, outer, acts, others, width, wide, add=sent)
        for bit in range(2, nb_bits):
            mine = (mine.astype(F32) + swap(mine, "batch", bit).astype(F32)).astype(BF)
        held, low = own_half(core, outer, mine, swap(mine, "batch", 1))
        return other_half(1 - core, outer, held, swap(low, "batch", 0))

    outer_w_sum = over_batch(True, (e0[0], e1[0]), (e0[2], e1[2]))
    inner_w_sum = over_batch(False, (e0[1], e1[1]), (e0[3], e1[3]))
    expert_rows = e0[7] + e1[7]
    biases = jnp.concatenate([expert_rows[1:2], (e0[6] + e1[6]).reshape(wide // width, width)], axis=0)
    for bit in range(nb_bits):
        biases = biases + swap(biases, "batch", bit)
    outer_b_sum = biases[:1]
    inner_b_sum = biases[1:].reshape(1, wide)

    stream_grad, attended_grad, second_grads, output_grad = return_stage(
        slots_row, tgt_col, in0, in1, stream, cotangent, small_t, att_t, gathered, gain_two_at
    )
    out0, out1, attended_grad = lax.optimization_barrier((e0[4], e1[4], attended_grad))
    outs = [exchange(out0), exchange(out1)]
    dq, dk, dv, wq, wk, wv = attend_back(mixed, attended_grad, lse, start_row, normed_t)
    input_grad, first_grads = last_stage(dq, dk, dv, gathered, tokens, stream_grad, small_t, gain_one_at)

    lane = lax.broadcasted_iota(jnp.int32, (width, LANES), 1)
    second_t = jnp.swapaxes(second_grads, 0, 1)
    router_col = jnp.swapaxes(expert_rows, 0, 1)[:, 0:1]
    small_two = jnp.where(
        lane == expert_here,
        router_col,
        jnp.where(lane == experts, second_t[:, 0:1], jnp.where(lane == experts + 1, second_t[:, 1:2], 0.0)),
    ).astype(BF)
    first_t = jnp.swapaxes(first_grads, 0, 1)
    small_one = jnp.where(lane == 0, first_t[:, 0:1], jnp.where(lane == 1, first_t[:, 1:2], 0.0)).astype(BF)
    summed_two = scatter_rows([output_grad, small_two], shard_rows)
    summed_one = scatter_rows([wq, wk, wv, small_one], shard_rows)

    block_output, result_sums = result_stage(slots_row, tgt_col, outs[0], outs[1], stream, gates)
    sums = sum_all(jnp.concatenate([second_sums[:2], result_sums[:2]], axis=0))
    gate_sums = sums[0, :experts]
    balance = jnp.sum((counts - average) / average * gate_sums) / total_tokens
    squares = jnp.stack([sums[2, 0], sums[1, 0], sums[3, 0]])
    root_means = jnp.sqrt(squares / (total_tokens * width) + 1e-06)

    return (
        block_output,
        input_grad,
        summed_one[:, : 3 * width],
        summed_two[:, :width],
        summed_one[:, 3 * width],
        summed_one[:, 3 * width + 1],
        summed_two[:, width + experts],
        summed_two[:, width + experts + 1],
        summed_two[:, width : width + experts],
        inner_w_sum,
        inner_b_sum,
        outer_w_sum,
        outer_b_sum,
        balance,
        root_means,
    )


def solution(mesh):
    everywhere = P(ANYWHERE, None)
    line = P(ANYWHERE)
    in_specs = (
        everywhere, everywhere, everywhere, everywhere, everywhere, everywhere, line, line, line, line, everywhere,
        P("expert", None, None), P("expert", None), P("expert", None, None), P("expert", None),
    )
    out_specs = (
        everywhere, everywhere, everywhere, everywhere, line, line, line, line, everywhere,
        P("expert", None, None), P("expert", None), P("expert", None, None), P("expert", None), P(), P(),
    )
    return jax.shard_map(shards, mesh=mesh, in_specs=in_specs, out_specs=out_specs, check_vma=False)
```

time: 978 us -> 659 us (0.67)
  matrix products: 327 us -> 0 us
  blocking collectives: 307 us -> 32.6 us
  Pallas kernels: 0 us -> 240 us
  waiting for transfers between devices: 92.2 us -> 235 us
  other arithmetic: 119 us -> 22.6 us
  starting transfers between devices: 12.4 us -> 66.5 us
  local copies, waits for them, and re-layouts: 86.6 us -> 48.4 us
  between operations: 16.8 us -> 3.44 us
    dot_general x29 -> x0, matrix products: 327 us -> none  [the longest x1 49.7 us: shards(): jnp.dot(received, inner_weight[0], preferred_element_type=jnp.float32)]
    pallas_call x0 -> x20, Pallas kernels: none -> 240 us  [the longest x2 60.5 us: expert_stage(): call(expert_body, 'expert', (wide // tile,), [pl.BlockSpec(memory_space=p...]
    ppermute x0 -> x22, waiting for transfers between devices: none -> 132 us  [swap(): return lax.ppermute(value, axis, [(i, i ^ 1 << bit) for i in range(size)])]
    all_gather x1 -> x0, blocking collectives: 109 us -> none  [shards(): lax.all_gather(router_weight, ('batch', 'expert'), axis=0, tiled=True)]
    unnamed x2 -> x0, blocking collectives: 83.3 us -> none
    psum x2 -> x0, blocking collectives: 59.1 us -> none  [the longest x1 48.7 us: shards(): lax.psum((local_counts, local_gates, local_squares), ('batch', 'expert'))]
    convert_element_type x13 -> x7, other arithmetic: 60.9 us -> 2.27 us  [the longest x1 0.95 us: shards(): small_t = gathered[:, 4 * width:].T.astype(F32)]
    all_to_all x3 -> x9, waiting for transfers between devices: 53.9 us -> 103 us  [the longest x7 91.7 us: exchange(): lax.all_to_all(shaped, 'expert', split_axis=0, concat_axis=0, tiled=True)]
  transfers between devices with their start and end apart: 8 -> 31, of which waited for: 3 -> 19; matrix products, arithmetic and copies ran while one was open for 41% -> 7% of each run, Pallas kernels for 0% -> 21%
where the time goes in v1:
time: 659 us; the launch traced here: 649 us
  Pallas kernels  240 us (36%)
  waiting for transfers between devices  235 us (36%)
  starting transfers between devices  66.5 us (10%)
  local copies, waits for them, and re-layouts  48.4 us (7%)
  blocking collectives  32.6 us (5%)
  other arithmetic  22.6 us (3%)
    ppermute x22, waiting for transfers between devices, swap(): return lax.ppermute(value, axis, [(i, i ^ 1 << bit) for i in range(size)])  132 us
    all_to_all x7, waiting for transfers between devices, exchange(): lax.all_to_all(shaped, 'expert', split_axis=0, concat_axis=0, tiled=True)  91.7 us
    pallas_call x2, Pallas kernels, expert_stage(): call(expert_body, 'expert', (wide // tile,), [pl.BlockSpec(memory_space=p...  60.5 us
    pallas_call x1, Pallas kernels, attend_back(): call(attend_back_body, 'attend_back', (PAIRS,), [full((1, rows)), column,...  39.1 us
    all_to_all x7, starting transfers between devices, exchange(): lax.all_to_all(shaped, 'expert', split_axis=0, concat_axis=0, tiled=True)  36.6 us
    all_to_all x1, blocking collectives, exchange(): lax.all_to_all(shaped, 'expert', split_axis=0, concat_axis=0, tiled=True)  32.6 us
    pallas_call x4, Pallas kernels, weight_grad(): call(outer_grad_body if outer else inner_grad_body, 'weight_grad', (steps...  31.4 us
    pallas_call x1, Pallas kernels, attend(): call(attend_body, 'attend', (PAIRS,), [full((1, rows)), pl.BlockSpec((row...  25.1 us
  transfers between devices with their start and end apart: 31, of which 19 were waited for; matrix products, arithmetic and copies ran while one was open for 7% of the time, Pallas kernels for 21%

profile of v1, /device:TPU:0, one launch (start us, length us, event | category | flops | bytes accessed | tf_op | source)
XLA Modules:
  0.0 648.6 jit_solution(9838632376738011353)
XLA Ops:
  14.1 7.3 %collective-permute-done = bf16[24,3200]{1,0:T(8,128)(2,1)S(1)} collective-permute-done((bf16[24,3200]{1,0:T(8,128)(2,1)S(1)}, bf16[24,3200]{1,0:T(8,128)(2,1)S(1)}, u32[]{:S(2)}, u32[]{:S(2)}) %collective-permute-start) | collective-permute-done | bytes 153632 | tf_op jit(solution)/shard_map/ppermute | solution.py:61
  22.2 7.7 %collective-permute-done.1 = bf16[2,24,3200]{2,1,0:T(8,128)(2,1)S(1)} collective-permute-done((bf16[2,24,3200]{2,1,0:T(8,128)(2,1)S(1)}, bf16[2,24,3200]{2,1,0:T(8,128)(2,1)S(1)}, u32[]{:S(2)}, u32[]{:S(2)}) %collective-permute-start.1) | collective-permute-done | bytes 307232 | tf_op jit(solution)/shard_map/ppermute | solution.py:61
  31.4 12.9 %collective-permute-done.2 = bf16[2,2,24,3200]{3,2,1,0:T(8,128)(2,1)S(1)} collective-permute-done((bf16[2,2,24,3200]{3,2,1,0:T(8,128)(2,1)S(1)}, bf16[2,2,24,3200]{3,2,1,0:T(8,128)(2,1)S(1)}, u32[]{:S(2)}, u32[]{:S(2)}) %collective-permute-start.2) | collective-permute-done | bytes 614432 | tf_op jit(solution)/shard_map/ppermute | solution.py:61
  46.8 25.3 %collective-permute-done.3 = bf16[2,2,2,24,3200]{4,3,2,1,0:T(8,128)(2,1)} collective-permute-done((bf16[2,2,2,24,3200]{4,3,2,1,0:T(8,128)(2,1)S(1)}, bf16[2,2,2,24,3200]{4,3,2,1,0:T(8,128)(2,1)}, u32[]{:S(2)}, u32[]{:S(2)}) %collective-permute-start.3) | collective-permute-done | bytes 1228832 | tf_op jit(solution)/shard_map/ppermute | solution.py:61
  75.5 7.0 %dispatch.2 = bf16[2,768,768]{2,1,0:T(8,128)(2,1)} custom-call(s32[1536,1]{1,0:T(8,128)} %constant.94.clone.slots, s32[1,1024]{1,0:T(1,128)} %get-tuple-element.68.tgt, bf16[1024,768]{1,0:T(8,128)(2,1)} %cot.1), custom_call_target="tpu_custom_call" | custom-call | flops 2415919104 | bytes 3932160 | tf_op jit(solution)/shard_map/dispatch/pallas_call | solution.py:162
  88.6 8.5 %first.1 = (bf16[1024,2304]{1,0:T(8,128)(2,1)}, bf16[768,1024]{1,0:T(8,128)(2,1)}) custom-call(bf16[1024,768]{1,0:T(8,128)(2,1)} %tokens.5, f32[128,768]{1,0:T(8,128)} %get-tuple-element.216.gains, bf16[768,3200]{1,0:T(8,128)(2,1)} %bitcast.128), custom_call_target="tpu_custom_call" | custom-call | flops 3623878656 | bytes 11403264 | tf_op jit(solution)/shard_map/first/pallas_call | solution.py:196
  97.1 25.1 %attend.1 = (bf16[1024,768]{1,0:T(8,128)(2,1)}, bf16[768,1024]{1,0:T(8,128)(2,1)}, f32[6,8,1024]{2,1,0:T(8,128)}) custom-call(s32[1,1024]{1,0:T(1,128)} %get-tuple-element.70.start, bf16[1024,2304]{1,0:T(8,128)(2,1)} %get-tuple-element.72.q.k.v, bf16[1024,2304]{1,0:T(8,128)(2,1)} %get-tuple-element.72.q.k.v, bf16[1024,2304]{1,0:T(8,128)(2,1)} %get-tuple-element.72.q.k.v), custom_call_target="tpu_custom_call" | custom-call | flops 6442450944 | bytes 7864320 | tf_op jit(solution)/shard_map/attend/pallas_call | solution.py:255
  122.2 8.6 %second.1 = (f32[1024,768]{1,0:T(8,128)}, bf16[1024,768]{1,0:T(8,128)(2,1)}, f32[1024,1]{1,0:T(8,128)}, f32[8,128]{1,0:T(8,128)}) custom-call(bf16[1024,768]{1,0:T(8,128)(2,1)} %get-tuple-element.73.att, bf16[768,3200]{1,0:T(8,128)(2,1)} %bitcast.129, bf16[1024,768]{1,0:T(8,128)(2,1)} %tokens.5, f32[128,768]{1,0:T(8,128)} %get-tuple-element.216.gains, ...), custom_call_target="tpu_custom_call" | custom-call | flops 1207959552 | bytes 9043968 | tf_op jit(solution)/shard_map/second/pallas_call | solution.py:368
  130.8 7.0 %dispatch.3 = bf16[2,768,768]{2,1,0:T(8,128)(2,1)} custom-call(s32[1536,1]{1,0:T(8,128)} %constant.94.clone.slots, s32[1,1024]{1,0:T(1,128)} %get-tuple-element.68.tgt, bf16[1024,768]{1,0:T(8,128)(2,1)} %get-tuple-element.74.x), custom_call_target="tpu_custom_call" | custom-call | flops 2415919104 | bytes 3932160 | tf_op jit(solution)/shard_map/dispatch/pallas_call | solution.py:162
  141.1 8.1 %all-to-all-start = ((bf16[8,96,768]{2,1,0:T(8,128)(2,1)}), bf16[8,96,768]{2,1,0:T(8,128)(2,1)}, u32[]{:S(2)}, u32[]{:S(2)}) async-start(bf16[8,96,768]{2,1,0:T(8,128)(2,1)} %bitcast.24), calls=%async_computation | async-start | bytes 2359296 | tf_op jit(solution)/shard_map/all_to_all | solution.py:734
  150.4 28.2 %all-to-all-done = bf16[8,96,768]{2,1,0:T(8,128)(2,1)} async-done(((bf16[8,96,768]{2,1,0:T(8,128)(2,1)}), bf16[8,96,768]{2,1,0:T(8,128)(2,1)}, u32[]{:S(2)}, u32[]{:S(2)}) %all-to-all-start) | async-done | bytes 1179680 | tf_op jit(solution)/shard_map/all_to_all | solution.py:734
  178.6 32.6 %all_to_all.50 = bf16[8,96,768]{2,1,0:T(8,128)(2,1)} all-to-all(bf16[8,96,768]{2,1,0:T(8,128)(2,1)S(1)} %bitcast.142), channel_id=1, replica_groups=mesh['batch'=4,'expert'=8] {'expert'}, dimensions={0} | all-to-all | bytes 2359296 | tf_op jit(solution)/shard_map/all_to_all | solution.py:734
  214.9 28.2 %all-to-all-done.1 = bf16[8,96,768]{2,1,0:T(8,128)(2,1)S(1)} async-done(((bf16[8,96,768]{2,1,0:T(8,128)(2,1)}), bf16[8,96,768]{2,1,0:T(8,128)(2,1)S(1)}, u32[]{:S(2)}, u32[]{:S(2)}) %all-to-all-start.1) | async-done | bytes 1179680 | tf_op jit(solution)/shard_map/all_to_all | solution.py:734
  246.9 6.7 %copy.132 = bf16[1,3072,768]{1,2,0:T(8,128)(2,1)} copy(bf16[1,3072,768]{2,1,0:T(8,128)(2,1)} %param.30) | data formatting | bytes 9437184 | tf_op args[13]
  253.5 6.6 %copy.133.w1t = bf16[3072,768]{1,0:T(8,128)(2,1)} copy(bf16[3072,768]{0,1:T(8,128)(2,1)} %bitcast.135) | data formatting | bytes 9437184 | tf_op jit(solution)/shard_map/transpose | solution.py:745
  265.3 30.3 %expert.2 = (bf16[3072,768]{1,0:T(8,128)(2,1)}, bf16[3072,768]{1,0:T(8,128)(2,1)}, bf16[768,768]{1,0:T(8,128)(2,1)}, bf16[768,768]{1,0:T(8,128)(2,1)}, bf16[768,...) custom-call(f32[1,1]{1,0:T(1,128)} %bitcast.22.bal, ...), custom_call_target="tpu_custom_call" | custom-call | flops 14495514624 | bytes 35389440 | tf_op jit(solution)/shard_map/expert/pallas_call | solution.py:434
  295.6 6.0 all-to-all-start.4
  301.5 30.2 %expert.3 = (bf16[3072,768]{1,0:T(8,128)(2,1)}, bf16[3072,768]{1,0:T(8,128)(2,1)}, bf16[768,768]{1,0:T(8,128)(2,1)}, bf16[768,768]{1,0:T(8,128)(2,1)}, bf16[768,...) custom-call(f32[1,1]{1,0:T(1,128)} %bitcast.22.bal, ...), custom_call_target="tpu_custom_call" | custom-call | flops 14495514624 | bytes 35389440 | tf_op jit(solution)/shard_map/expert/pallas_call | solution.py:434
  331.8 6.2 all-to-all-start.5
  339.3 26.6 %all-to-all-done.5 = bf16[8,96,768]{2,1,0:T(8,128)(2,1)S(1)} async-done(((bf16[8,96,768]{2,1,0:T(8,128)(2,1)}), bf16[8,96,768]{2,1,0:T(8,128)(2,1)S(1)}, u32[]{:S(2)}, u32[]{:S(2)}) %all-to-all-start.5) | async-done | bytes 1179680 | tf_op jit(solution)/shard_map/all_to_all | solution.py:734
  366.9 13.2 %return.1 = (f32[1024,768]{1,0:T(8,128)}, bf16[1024,768]{1,0:T(8,128)(2,1)}, f32[8,768]{1,0:T(8,128)}, bf16[768,768]{1,0:T(8,128)(2,1)}) custom-call(s32[2,768]{1,0:T(2,128)} %constant.93.clone.slots, s32[1024,1]{1,0:T(8,128)} %copy.140.tgt, bf16[768,768]{1,0:T(8,128)(2,1)} %bitcast.158, bf16[768,768]{1,0:T(8,128)(2,1)} %bitcast.162, ...), custom_call_target="tpu_custom_call" | custom-call | flops 4831838208 | bytes 14942208 | tf_op jit(solution)/shard_map/return/pallas_call | solution.py:603
  381.6 39.1 %attend_back.1 = (bf16[1024,768]{1,0:T(8,128)(2,1)}, bf16[1024,768]{1,0:T(8,128)(2,1)}, bf16[1024,768]{1,0:T(8,128)(2,1)}, bf16[768,768]{1,0:T(8,128)(2,1)}, bf1...) custom-call(s32[1,1024]{1,0:T(1,128)} %get-tuple-element.70.start, bf16[1024,2304]{1,0:T(8,128)(2,1)} %get-tuple-element.72.q.k.v, ...), custom_call_target="tpu_custom_call" | custom-call | flops 16106127360 | bytes 15728640 | tf_op jit(solution)/shard_map/attend_back/pallas_call | solution.py:315
  429.0 7.5 %weight_grad.6 = bf16[1536,768]{1,0:T(8,128)(2,1)} custom-call(s32[1]{0:T(128)S(6)} %sub.21.core.which, bf16[3072,768]{1,0:T(8,128)(2,1)} %get-tuple-element.113.a0, bf16[3072,768]{1,0:T(8,128)(2,1)} %get-tuple-element.114.a1, bf16[768,768]{1,0:T(8,128)(2,1)} %get-tuple-element.115.g0, bf16[768,768]{1,0:T(8,128)(2,1)} %get-tuple-element.116.g1), custom_call_target="tpu_custom_call" | custom-call | flops 3623878656 | bytes 11796480 | tf_op jit(solution)/shard_map/weight_grad/pallas_call | solution.py:511
  436.6 10.9 %all-to-all-done.9 = bf16[8,2,24,896]{3,2,1,0:T(8,128)(2,1)S(1)} async-done(((bf16[8,2,24,896]{3,2,1,0:T(8,128)(2,1)}), bf16[8,2,24,896]{3,2,1,0:T(8,128)(2,1)S(1)}, u32[]{:S(2)}, u32[]{:S(2)}) %all-to-all-start.9) | async-done | bytes 688160 | tf_op jit(solution)/shard_map/all_to_all | solution.py:102
  452.0 7.5 %weight_grad.4 = bf16[768,1536]{1,0:T(8,128)(2,1)} custom-call(s32[1]{0:T(128)S(6)} %sub.21.core.which, bf16[3072,768]{1,0:T(8,128)(2,1)} %get-tuple-element.105.a0, bf16[3072,768]{1,0:T(8,128)(2,1)} %get-tuple-element.106.a1, bf16[768,768]{1,0:T(8,128)(2,1)} %get-tuple-element.107.x0, bf16[768,768]{1,0:T(8,128)(2,1)} %get-tuple-element.108.x1), custom_call_target="tpu_custom_call" | custom-call | flops 3623878656 | bytes 11796480 | tf_op jit(solution)/shard_map/weight_grad/pallas_call | solution.py:511
  463.9 10.1 %last.1 = (f32[1024,768]{1,0:T(8,128)}, f32[8,768]{1,0:T(8,128)}) custom-call(bf16[1024,768]{1,0:T(8,128)(2,1)} %get-tuple-element.92.dq, bf16[1024,768]{1,0:T(8,128)(2,1)} %get-tuple-element.93.dk, bf16[1024,768]{1,0:T(8,128)(2,1)} %get-tuple-element.94.dv, bf16[768,3200]{1,0:T(8,128)(2,1)} %bitcast.132, bf16[768,3200]{1,0:T(8,128)(2,1)} %bitcast.133, ...), custom_call_target="tpu_custom_call" | custom-call | flops 3623878656 | bytes 16121856 | tf_op jit(solution)/shard_map/last/pallas_call | solution.py:646
  484.7 8.2 %weight_grad.7.a = bf16[1536,768]{1,0:T(8,128)(2,1)} custom-call(s32[1]{0:T(128)} %bitcast.71.core.which, bf16[3072,768]{1,0:T(8,128)(2,1)} %get-tuple-element.113.a0, bf16[3072,768]{1,0:T(8,128)(2,1)} %get-tuple-element.114.a1, bf16[768,768]{1,0:T(8,128)(2,1)} %get-tuple-element.115.g0, bf16[768,768]{1,0:T(8,128)(2,1)} %get-tuple-element.116.g1, ...), custom_call_target="tpu_custom_call" | custom-call | flops 3623878656 | bytes 11796480 | tf_op jit(solution)/shard_map/weight_grad/pallas_call | solution.py:511
  494.4 8.2 %weight_grad.5.a = bf16[768,1536]{1,0:T(8,128)(2,1)} custom-call(s32[1]{0:T(128)} %bitcast.71.core.which, bf16[3072,768]{1,0:T(8,128)(2,1)} %get-tuple-element.105.a0, bf16[3072,768]{1,0:T(8,128)(2,1)} %get-tuple-element.106.a1, bf16[768,768]{1,0:T(8,128)(2,1)} %get-tuple-element.107.x0, bf16[768,768]{1,0:T(8,128)(2,1)} %get-tuple-element.108.x1, ...), custom_call_target="tpu_custom_call" | custom-call | flops 3623878656 | bytes 11796480 | tf_op jit(solution)/shard_map/weight_grad/pallas_call | solution.py:511
  506.3 7.0 %all-to-all-done.7 = bf16[8,96,768]{2,1,0:T(8,128)(2,1)} async-done(((bf16[8,96,768]{2,1,0:T(8,128)(2,1)}), bf16[8,96,768]{2,1,0:T(8,128)(2,1)}, u32[]{:S(2)}, u32[]{:S(2)}) %all-to-all-start.7) | async-done | bytes 1179680 | tf_op jit(solution)/shard_map/all_to_all | solution.py:734
  519.4 27.9 %collective-permute-done.15.b = bf16[1536,768]{1,0:T(8,128)(2,1)} collective-permute-done((bf16[1536,768]{1,0:T(8,128)(2,1)}, bf16[1536,768]{1,0:T(8,128)(2,1)}, u32[]{:S(2)}, u32[]{:S(2)}) %collective-permute-start.15) | collective-permute-done | bytes 2359328 | tf_op jit(solution)/shard_map/ppermute | solution.py:61
  553.2 43.3 %collective-permute-done.10.b = bf16[768,1536]{1,0:T(8,128)(2,1)} collective-permute-done((bf16[768,1536]{1,0:T(8,128)(2,1)}, bf16[768,1536]{1,0:T(8,128)(2,1)}, u32[]{:S(2)}, u32[]{:S(2)}) %collective-permute-start.10) | collective-permute-done | bytes 2359328 | tf_op jit(solution)/shard_map/ppermute | solution.py:61
  606.4 7.3 %result.1 = (bf16[1024,768]{1,0:T(8,128)(2,1)}, f32[8,128]{1,0:T(8,128)}) custom-call(s32[2,768]{1,0:T(2,128)} %constant.93.clone.slots, s32[1024,1]{1,0:T(8,128)} %copy.140.tgt, bf16[768,768]{1,0:T(8,128)(2,1)} %bitcast.45.r0, bf16[768,768]{1,0:T(8,128)(2,1)} %bitcast.47.r1, f32[1024,768]{1,0:T(8,128)} %get-tuple-element.82.stream, ...), custom_call_target="tpu_custom_call" | custom-call | flops 2415919104 | bytes 7864320 | tf_op jit(solution)/shard_map/result/pallas_call | solution.py:676
  (182 shorter events, 135.8 us)
Async XLA Ops:
  10.0 11.4 %collective-permute-start = (bf16[24,3200]{1,0:T(8,128)(2,1)S(1)}, bf16[24,3200]{1,0:T(8,128)(2,1)S(1)}, u32[]{:S(2)}, u32[]{:S(2)}) collective-permute-start(bf16[24,3200]{1,0:T(8,128)(2,1)S(1)} %concatenate.21), channel_id=1, source_target_pairs={{0,4},{1,5},{2,6},{3,7},{4,0},{5,1},{6,2},{7,3},{8,12},{9,13},{10,... | collective-permute-start | bytes 460808 | tf_op jit(solution)/shard_map/ppermute | solution.py:61
  21.4 8.5 %collective-permute-start.1 = (bf16[2,24,3200]{2,1,0:T(8,128)(2,1)S(1)}, bf16[2,24,3200]{2,1,0:T(8,128)(2,1)S(1)}, u32[]{:S(2)}, u32[]{:S(2)}) collective-permute-start(bf16[2,24,3200]{2,1,0:T(8,128)(2,1)S(1)} %pad_maximum_fusion.6), channel_id=1, source_target_pairs={{0,2},{1,3},{2,0},{3,1},{4,6},{5,7},{6,4},{7,5},{8,10},{9,11},{10,... | collective-permute-start | bytes 921608 | tf_op jit(solution)/shard_map/ppermute | solution.py:61
  30.1 14.2 %collective-permute-start.2 = (bf16[2,2,24,3200]{3,2,1,0:T(8,128)(2,1)S(1)}, bf16[2,2,24,3200]{3,2,1,0:T(8,128)(2,1)S(1)}, u32[]{:S(2)}, u32[]{:S(2)}) collective-permute-start(bf16[2,2,24,3200]{3,2,1,0:T(8,128)(2,1)S(1)} %pad_maximum_fusion.5), channel_id=1, source_target_pairs={{0,1},{1,0},{2,3},{3,2},{4,5},{5,4},{6,7},{7,6},{8,9},{9,8},{10,11... | collective-permute-start | bytes 1843208 | tf_op jit(solution)/shard_map/ppermute | solution.py:61
  45.4 26.6 %collective-permute-start.3 = (bf16[2,2,2,24,3200]{4,3,2,1,0:T(8,128)(2,1)S(1)}, bf16[2,2,2,24,3200]{4,3,2,1,0:T(8,128)(2,1)}, u32[]{:S(2)}, u32[]{:S(2)}) collective-permute-start(bf16[2,2,2,24,3200]{4,3,2,1,0:T(8,128)(2,1)S(1)} %pad_maximum_fusion.3), channel_id=1, source_target_pairs={{0,16},{8,24},{16,0},{24,8},{1,17},{9,25},{17,1},{25,9},{2,18},{10... | collective-permute-start | bytes 3686408 | tf_op jit(solution)/shard_map/ppermute | solution.py:61
  75.5 7.0 %collective-permute-start.4 = (bf16[2,2,2,2,24,3200]{5,4,3,2,1,0:T(8,128)(2,1)}, bf16[2,2,2,2,24,3200]{5,4,3,2,1,0:T(8,128)(2,1)}, u32[]{:S(2)}, u32[]{:S(2)}) collective-permute-start(bf16[2,2,2,2,24,3200]{5,4,3,2,1,0:T(8,128)(2,1)} %pad_maximum_fusion.1), channel_id=1, source_target_pairs={{0,8},{8,0},{16,24},{24,16},{1,9},{9,1},{17,25},{25,17},{2,10},{10... | collective-permute-start | bytes 7372808 | tf_op jit(solution)/shard_map/ppermute | solution.py:61
  141.1 37.5 %all-to-all-start = ((bf16[8,96,768]{2,1,0:T(8,128)(2,1)}), bf16[8,96,768]{2,1,0:T(8,128)(2,1)}, u32[]{:S(2)}, u32[]{:S(2)}) async-start(bf16[8,96,768]{2,1,0:T(8,128)(2,1)} %bitcast.24), calls=%async_computation | async-start | bytes 2359296 | tf_op jit(solution)/shard_map/all_to_all | solution.py:734
  211.2 31.9 %all-to-all-start.1 = ((bf16[8,96,768]{2,1,0:T(8,128)(2,1)}), bf16[8,96,768]{2,1,0:T(8,128)(2,1)S(1)}, u32[]{:S(2)}, u32[]{:S(2)}) async-start(bf16[8,96,768]{2,1,0:T(8,128)(2,1)} %bitcast.26), calls=%async_computation.1 | async-start | bytes 2359296 | tf_op jit(solution)/shard_map/all_to_all | solution.py:734
  243.1 52.4 %all-to-all-start.2 = ((bf16[8,96,768]{2,1,0:T(8,128)(2,1)}), bf16[8,96,768]{2,1,0:T(8,128)(2,1)S(1)}, u32[]{:S(2)}, u32[]{:S(2)}) async-start(bf16[8,96,768]{2,1,0:T(8,128)(2,1)} %bitcast.35), calls=%async_computation.2 | async-start | bytes 2359296 | tf_op jit(solution)/shard_map/all_to_all | solution.py:734
  295.6 36.3 %all-to-all-start.4 = ((bf16[8,96,768]{2,1,0:T(8,128)(2,1)}), bf16[8,96,768]{2,1,0:T(8,128)(2,1)S(1)}, u32[]{:S(2)}, u32[]{:S(2)}) async-start(bf16[8,96,768]{2,1,0:T(8,128)(2,1)} %bitcast.163), calls=%async_computation.4 | async-start | bytes 2359296 | tf_op jit(solution)/shard_map/all_to_all | solution.py:734
  331.8 34.0 %all-to-all-start.5 = ((bf16[8,96,768]{2,1,0:T(8,128)(2,1)}), bf16[8,96,768]{2,1,0:T(8,128)(2,1)S(1)}, u32[]{:S(2)}, u32[]{:S(2)}) async-start(bf16[8,96,768]{2,1,0:T(8,128)(2,1)} %bitcast.160), calls=%async_computation.5 | async-start | bytes 2359296 | tf_op jit(solution)/shard_map/all_to_all | solution.py:734
  381.6 39.1 %copy-start.4 = (bf16[768,768]{1,0:T(8,128)(2,1)S(1)}, bf16[768,768]{1,0:T(8,128)(2,1)}, u32[]{:S(2)}) copy-start(bf16[768,768]{1,0:T(8,128)(2,1)} %get-tuple-element.101) | copy-start | bytes 3538948
  422.2 2.2 collective-permute-start.7
  425.4 22.1 %all-to-all-start.9 = ((bf16[8,2,24,896]{3,2,1,0:T(8,128)(2,1)}), bf16[8,2,24,896]{3,2,1,0:T(8,128)(2,1)S(1)}, u32[]{:S(2)}, u32[]{:S(2)}) async-start(bf16[8,2,24,896]{3,2,1,0:T(8,128)(2,1)} %fusion.1), calls=%async_computation.9 | async-start | bytes 1376256 | tf_op jit(solution)/shard_map/all_to_all | solution.py:102
  436.4 48.3 %collective-permute-start.14 = (bf16[1536,768]{1,0:T(8,128)(2,1)}, bf16[1536,768]{1,0:T(8,128)(2,1)}, u32[]{:S(2)}, u32[]{:S(2)}) collective-permute-start(bf16[1536,768]{1,0:T(8,128)(2,1)} %weight_grad.6), channel_id=1, source_target_pairs={{0,8},{8,0},{16,24},{24,16},{1,9},{9,1},{17,25},{25,17},{2,10},{10... | collective-permute-start | bytes 7077896 | tf_op jit(solution)/shard_map/ppermute | solution.py:61
  447.5 32.8 %all-to-all-start.6 = ((bf16[8,96,768]{2,1,0:T(8,128)(2,1)}), bf16[8,96,768]{2,1,0:T(8,128)(2,1)}, u32[]{:S(2)}, u32[]{:S(2)}) async-start(bf16[8,96,768]{2,1,0:T(8,128)(2,1)} %bitcast.156), calls=%async_computation.6 | async-start | bytes 2359296 | tf_op jit(solution)/shard_map/all_to_all | solution.py:734
  459.5 34.9 %collective-permute-start.9 = (bf16[768,1536]{1,0:T(8,128)(2,1)}, bf16[768,1536]{1,0:T(8,128)(2,1)}, u32[]{:S(2)}, u32[]{:S(2)}) collective-permute-start(bf16[768,1536]{1,0:T(8,128)(2,1)} %weight_grad.4), channel_id=1, source_target_pairs={{0,8},{8,0},{16,24},{24,16},{1,9},{9,1},{17,25},{25,17},{2,10},{10... | collective-permute-start | bytes 7077896 | tf_op jit(solution)/shard_map/ppermute | solution.py:61
  478.0 25.2 %collective-permute-start.5 = (bf16[2,8,24,2432]{3,2,0,1:T(8,128)(2,1)}, bf16[2,8,24,2432]{3,2,0,1:T(8,128)(2,1)}, u32[]{:S(2)}, u32[]{:S(2)}) collective-permute-start(bf16[2,8,24,2432]{3,2,0,1:T(8,128)(2,1)} %pad_maximum_fusion.2), channel_id=1, source_target_pairs={{0,8},{8,0},{16,24},{24,16},{1,9},{9,1},{17,25},{25,17},{2,10},{10... | collective-permute-start | bytes 5603336 | tf_op jit(solution)/shard_map/ppermute | solution.py:61
  480.3 33.0 %all-to-all-start.7 = ((bf16[8,96,768]{2,1,0:T(8,128)(2,1)}), bf16[8,96,768]{2,1,0:T(8,128)(2,1)}, u32[]{:S(2)}, u32[]{:S(2)}) async-start(bf16[8,96,768]{2,1,0:T(8,128)(2,1)} %bitcast.155), calls=%async_computation.7 | async-start | bytes 2359296 | tf_op jit(solution)/shard_map/all_to_all | solution.py:734
  492.9 54.4 %collective-permute-start.15 = (bf16[1536,768]{1,0:T(8,128)(2,1)}, bf16[1536,768]{1,0:T(8,128)(2,1)}, u32[]{:S(2)}, u32[]{:S(2)}) collective-permute-start(bf16[1536,768]{1,0:T(8,128)(2,1)} %weight_grad.7.a), channel_id=1, source_target_pairs={{0,16},{8,24},{16,0},{24,8},{1,17},{9,25},{17,1},{25,9},{2,18},{10... | collective-permute-start | bytes 7077896 | tf_op jit(solution)/shard_map/ppermute | solution.py:61
  502.6 93.9 %collective-permute-start.10 = (bf16[768,1536]{1,0:T(8,128)(2,1)}, bf16[768,1536]{1,0:T(8,128)(2,1)}, u32[]{:S(2)}, u32[]{:S(2)}) collective-permute-start(bf16[768,1536]{1,0:T(8,128)(2,1)} %weight_grad.5.a), channel_id=1, source_target_pairs={{0,16},{8,24},{16,0},{24,8},{1,17},{9,25},{17,1},{25,9},{2,18},{10... | collective-permute-start | bytes 7077896 | tf_op jit(solution)/shard_map/ppermute | solution.py:61
  513.3 117.6 %all-to-all-start.8 = ((bf16[8,2,24,2432]{3,2,1,0:T(8,128)(2,1)}), bf16[8,2,24,2432]{3,2,1,0:T(8,128)(2,1)S(1)}, u32[]{:S(2)}, u32[]{:S(2)}) async-start(bf16[8,2,24,2432]{3,2,1,0:T(8,128)(2,1)} %fusion), calls=%async_computation.8 | async-start | bytes 3735552 | tf_op jit(solution)/shard_map/all_to_all | solution.py:102
  519.4 83.1 %collective-permute-start.12 = (f32[5,768]{1,0:T(8,128)S(1)}, f32[5,768]{1,0:T(8,128)S(1)}, u32[]{:S(2)}, u32[]{:S(2)}) collective-permute-start(f32[5,768]{1,0:T(8,128)S(1)} %pad_maximum_fusion.7), channel_id=1, source_target_pairs={{0,8},{8,0},{16,24},{24,16},{1,9},{9,1},{17,25},{25,17},{2,10},{10... | collective-permute-start | bytes 46088 | tf_op jit(solution)/shard_map/ppermute | solution.py:61
  553.2 83.9 %collective-permute-start.16 = (bf16[1536,768]{1,0:T(8,128)(2,1)}, bf16[1536,768]{1,0:T(8,128)(2,1)}, u32[]{:S(2)}, u32[]{:S(2)}) collective-permute-start(bf16[1536,768]{1,0:T(8,128)(2,1)} %get-tuple-element.118), channel_id=1, source_target_pairs={{0,8},{8,0},{16,24},{24,16},{1,9},{9,1},{17,25},{25,17},{2,10},{10... | collective-permute-start | bytes 7077896 | tf_op jit(solution)/shard_map/ppermute | solution.py:61
  602.5 38.9 %collective-permute-start.11 = (bf16[768,1536]{1,0:T(8,128)(2,1)}, bf16[768,1536]{1,0:T(8,128)(2,1)}, u32[]{:S(2)}, u32[]{:S(2)}) collective-permute-start(bf16[768,1536]{1,0:T(8,128)(2,1)} %get-tuple-element.110), channel_id=1, source_target_pairs={{0,8},{8,0},{16,24},{24,16},{1,9},{9,1},{17,25},{25,17},{2,10},{10... | collective-permute-start | bytes 7077896 | tf_op jit(solution)/shard_map/ppermute | solution.py:61
  602.5 3.9 collective-permute-start.13
  614.4 3.6 collective-permute-start.17
  618.0 3.7 collective-permute-start.18
  619.8 6.3 collective-permute-start.8
  621.7 4.5 collective-permute-start.19
  626.2 1.2 collective-permute-start.20
  627.3 3.6 collective-permute-start.21
  631.2 14.4 %collective-permute-start.6 = (f32[1,24,2432]{2,1,0:T(8,128)S(1)}, f32[1,24,2432]{2,1,0:T(8,128)S(1)}, u32[]{:S(2)}, u32[]{:S(2)}) collective-permute-start(f32[1,24,2432]{2,1,0:T(8,128)S(1)} %constant_dynamic-slice_fusion.3), channel_id=1, source_target_pairs={{0,16},{8,24},{16,0},{24,8},{1,17},{9,25},{17,1},{25,9},{2,18},{10... | collective-permute-start | bytes 700424 | tf_op jit(solution)/shard_map/ppermute | solution.py:61
  (13 other events, 139.2 us)
